TPU v7x, 256 devices: a whole 4x4x8 slice. The times are simulated.
256 devices in a mesh: seq: 64 (over z, x, core), rep: 4 (over y).
Axes of the slice: x: 4, y: 4, z: 8, core: 2. Of those that a mesh axis runs over, the one named last changes fastest.
Arguments:
- queries: bfloat16 [32768, 8192], P(('rep', 'seq')), may hold values from -6 to 6
- keys: bfloat16 [32768, 1024], P(('rep', 'seq')), may hold values from -6 to 6
- values: bfloat16 [32768, 1024], P(('rep', 'seq')), may hold values from -6 to 6
- vertical: int32 [64, 24], replicated, may hold values from -1 to 511, as said below
- slash: int32 [64, 24], replicated, may hold values from -1 to 511, as said below
Outputs:
- attention: bfloat16 [32768, 8192], P(('rep', 'seq'))
Inputs may be any that keep to these rules, and one draw needn't show every extreme that they name: `vertical`: in each row the entries other than -1 come first and are distinct; every row has at least one; some row has all 24 in use. `slash`: each row begins with 0; the entries other than -1 come first and are distinct; some row has all 24 in use.
All inputs are finite; a program needn't handle non-finite values.
Results may differ from a plain program's by a relative error of at most 0.0055.
Values may be sent and summed in bfloat16 or wider, within the bound.
No kernel may reach another device: no remote copies, remote signals or barrier semaphores. Data moves between devices by JAX's collectives and lax.ppermute only.
A program may use at most 128 MiB of HBM per device.

v0:
```python
import functools
import math

import jax
import jax.numpy as jnp
from jax import lax
from jax.experimental import pallas as pl
from jax.experimental.pallas import tpu as pltpu
from jax.sharding import Mesh, PartitionSpec as P

QUERY_HEADS = 64
KEY_VALUE_HEADS = 8
HEADS = QUERY_HEADS // KEY_VALUE_HEADS
HEAD_SIZE = 128
BLOCK = 64
ROWS = 128
SLOTS = 48
TILES = 8
CHUNK = 8
NEG_FILL = -1e30
SCALE = math.log2(math.e) / math.sqrt(HEAD_SIZE)


def attend_kernel(
    tiles, idx_ref, count_ref, query_ref, key_hbm, value_hbm, out_ref, keys, values, score_s, sem
):
    width = CHUNK * BLOCK
    key_copy = pltpu.make_async_copy(key_hbm, keys, sem.at[0])
    value_copy = pltpu.make_async_copy(value_hbm, values, sem.at[1])
    key_copy.start()
    value_copy.start()
    key_copy.wait()
    lane = lax.broadcasted_iota(jnp.int32, (BLOCK, width), 1)
    row = lax.broadcasted_iota(jnp.int32, (BLOCK, width), 0)
    causal = (lane >= BLOCK) | (lane <= row)
    groups = tiles // TILES

    def fold(op, x):
        return functools.reduce(op, [x[:, a : a + 128] for a in range(0, width, 128)])

    def group(step, _):
        head = step // groups
        first_tile = (step % groups) * TILES
        lanes = pl.ds(pl.multiple_of(head * HEAD_SIZE, HEAD_SIZE), HEAD_SIZE)
        rows = [pl.ds((first_tile + t) * BLOCK, BLOCK) for t in range(TILES)]
        lists = [head * tiles + first_tile + t for t in range(TILES)]
        counts = [count_ref[x] for x in lists]
        chunks = (functools.reduce(jnp.maximum, counts) + CHUNK - 1) // CHUNK
        query = [query_ref[r, lanes] for r in rows]

        def gathered(ref, t, c):
            starts = [pl.multiple_of(idx_ref[lists[t], c * CHUNK + j], BLOCK) for j in range(CHUNK)]
            return jnp.concatenate([ref[pl.ds(s, BLOCK), :] for s in starts], axis=0)

        def score(c, best, first):
            out = []
            for t in range(TILES):
                s = lax.dot_general(
                    query[t],
                    gathered(keys, t, c),
                    (((1,), (1,)), ((), ())),
                    preferred_element_type=jnp.float32,
                )
                ok = lane < (counts[t] - c * CHUNK) * BLOCK
                if first:
                    ok = ok & causal
                s = jnp.where(ok, s, NEG_FILL)
                score_s[t, c] = s
                top = fold(jnp.maximum, s)
                out.append(top if first else jnp.maximum(best[t], top))
            return tuple(out)

        best = score(0, None, True)
        best = lax.fori_loop(1, chunks, lambda c, b: score(c, b, False), best)
        shift = [jnp.max(b, axis=1, keepdims=True) * SCALE for b in best]

        @pl.when(step == 0)
        def _():
            value_copy.wait()

        def mix(c, carried, first):
            out = []
            for t in range(TILES):
                p = jnp.exp2(score_s[t, c] * SCALE - shift[t])
                total = fold(jnp.add, p)
                mixed = jnp.dot(
                    p.astype(jnp.bfloat16),
                    gathered(values, t, c),
                    preferred_element_type=jnp.float32,
                )
                out.append(
                    (total, mixed) if first else (carried[t][0] + total, carried[t][1] + mixed)
                )
            return tuple(out)

        state = mix(0, None, True)
        state = lax.fori_loop(1, chunks, lambda c, s: mix(c, s, False), state)
        for t in range(TILES):
            total, mixed = state[t]
            share = 1.0 / jnp.sum(total, axis=1, keepdims=True)
            out_ref[rows[t], lanes] = (mixed * share).astype(jnp.bfloat16)
        return 0

    lax.fori_loop(0, HEADS * groups, group, 0)


def attend(idx, count, query_rows, key_rows, value_rows):
    tiles = query_rows.shape[0] // BLOCK
    tokens = key_rows.shape[0]
    smem = pl.BlockSpec(memory_space=pltpu.SMEM)
    vmem = pl.BlockSpec(memory_space=pltpu.VMEM)
    hbm = pl.BlockSpec(memory_space=pl.ANY)
    return pl.pallas_call(
        functools.partial(attend_kernel, tiles),
        out_shape=jax.ShapeDtypeStruct(query_rows.shape, jnp.bfloat16),
        in_specs=[smem, smem, vmem, hbm, hbm],
        out_specs=vmem,
        scratch_shapes=[
            pltpu.VMEM((tokens, HEAD_SIZE), jnp.bfloat16),
            pltpu.VMEM((tokens, HEAD_SIZE), jnp.bfloat16),
            pltpu.VMEM((TILES, SLOTS // CHUNK, BLOCK, CHUNK * BLOCK), jnp.float32),
            pltpu.SemaphoreType.DMA((2,)),
        ],
        compiler_params=pltpu.CompilerParams(vmem_limit_bytes=40 << 20),
    )(idx, count, query_rows, key_rows, value_rows)


def block_lists(vertical, slash, sizes):
    planes, across, cores, _ = sizes
    z, x = lax.axis_index("z"), lax.axis_index("x")
    core, y = lax.axis_index("core"), lax.axis_index("rep")
    per = ROWS // BLOCK
    tiles = planes * per
    columns = lax.dynamic_slice_in_dim(vertical, z * HEADS, HEADS, 0)
    offsets = lax.dynamic_slice_in_dim(slash, z * HEADS, HEADS, 0)
    tile = jnp.arange(tiles, dtype=jnp.int32)
    strip = ((y * planes + tile // per) * across + x) * cores + core
    blocks = strip * per + tile % per
    sources = blocks[None, :, None] - offsets[:, None, :]
    repeated = jnp.any(sources[..., None] == columns[:, None, None, :], axis=-1)
    keep_source = (offsets >= 0)[:, None, :] & (sources >= 0)
    keep_source &= (offsets == 0)[:, None, :] | ~repeated
    spread = jnp.broadcast_to(columns[:, None, :], sources.shape)
    keep_column = (spread >= 0) & (spread < blocks[None, :, None])
    picks = jnp.concatenate([sources, spread], axis=-1).reshape(HEADS * tiles, SLOTS)
    keep = jnp.concatenate([keep_source, keep_column], axis=-1).reshape(HEADS * tiles, SLOTS)
    slot = jnp.arange(SLOTS, dtype=jnp.int32)
    place = jnp.sum((keep[:, None, :] & (slot[None, :] < slot[:, None])[None]).astype(jnp.int32), -1)
    half = picks % per
    strip = picks // per
    core_of = strip % cores
    x_of = strip // cores % across
    z_of = strip // (cores * across) % planes
    y_of = strip // (cores * across * planes)
    where = ((((y_of * across + x_of) * cores + core_of) * planes + z_of) * per + half) * BLOCK
    hit = keep[:, None, :] & (place[:, None, :] == slot[None, :, None])
    idx = jnp.sum(jnp.where(hit, where[:, None, :], 0), axis=-1)
    return idx, jnp.sum(keep.astype(jnp.int32), axis=-1)


def body(sizes, queries, keys, values, vertical, slash):
    planes = sizes[0]
    idx, count = block_lists(vertical, slash, sizes)

    def regroup(x):
        x = x.reshape(ROWS, planes, -1).transpose(1, 0, 2)
        return lax.all_to_all(x, "z", split_axis=0, concat_axis=0, tiled=True)

    def whole(x):
        x = regroup(x).reshape(planes * ROWS, HEAD_SIZE)
        return lax.all_gather(x, ("rep", "x", "core"), axis=0, tiled=True)

    key_rows, value_rows = whole(keys), whole(values)
    query_rows = regroup(queries).reshape(planes * ROWS, HEADS * HEAD_SIZE)
    out = attend(idx, count, query_rows, key_rows, value_rows)
    out = lax.all_to_all(
        out.reshape(planes, ROWS, HEADS * HEAD_SIZE), "z", split_axis=0, concat_axis=0, tiled=True
    )
    return out.transpose(1, 0, 2).reshape(ROWS, QUERY_HEADS * HEAD_SIZE)


def solution(mesh):
    reps = mesh.devices.shape[1]
    sizes = (8, 4, 2, reps)
    split = Mesh(mesh.devices.reshape(sizes), ("z", "x", "core", "rep"))
    rows = P(("rep", "z", "x", "core"), None)
    return jax.shard_map(
        functools.partial(body, sizes),
        mesh=split,
        in_specs=(rows, rows, rows, P(), P()),
        out_specs=rows,
        check_vma=False,
    )
```

profile of v0, /device:TPU:30, one launch (start us, length us, event | category | flops | bytes accessed | tf_op | source)
XLA Modules:
  0.0 266.2 jit_solution(7212755576001462419)
XLA Ops:
  6.5 0.9 copy-done
  7.5 20.2 %all_to_all.20 = bf16[8,128,128]{2,1,0:T(8,128)(2,1)} all-to-all(bf16[8,128,128]{2,1,0:T(8,128)(2,1)S(1)} %bitcast_bitcast_fusion.2), channel_id=1, replica_groups=mesh['z'=8,'x'=4,'core'=2,'rep'=4] {'z'}, dimensions={0} | all-to-all | bytes 524288 | tf_op jit(solution)/shard_map/all_to_all | solution.py:167
  27.9 1.0 bitcast_bitcast_fusion.1
  28.9 13.5 %all_to_all.21 = bf16[8,128,128]{2,1,0:T(8,128)(2,1)} all-to-all(bf16[8,128,128]{2,1,0:T(8,128)(2,1)S(1)} %bitcast_bitcast_fusion.1), channel_id=1, replica_groups=mesh['z'=8,'x'=4,'core'=2,'rep'=4] {'z'}, dimensions={0} | all-to-all | bytes 524288 | tf_op jit(solution)/shard_map/all_to_all | solution.py:167
  42.4 1.6 copy.62
  44.0 3.7 %all-to-all-start = ((bf16[8,128,1024]{2,1,0:T(8,128)(2,1)}), bf16[8,128,1024]{2,1,0:T(8,128)(2,1)S(1)}, u32[]{:S(2)}, u32[]{:S(2)}) async-start(bf16[8,128,1024]{2,1,0:T(8,128)(2,1)} %bitcast.52), calls=%async_computation | async-start | bytes 4194304 | tf_op jit(solution)/shard_map/all_to_all | solution.py:167
  48.0 0.1 copy.44
  48.2 2.8 %compare_reduce_fusion = pred[8,16,24]{2,1,0:T(8,128)(4,1)S(1)} fusion(s32[8,24]{1,0:T(8,128)S(1)} %copy.45, s32[8,16,24]{2,1,0:T(8,128)S(1)} %broadcast_subtract_fusion), kind=kLoop, calls=%fused_computation.1 | loop fusion | flops 144384 | bytes 16128 | tf_op jit(solution)/shard_map/reduce_or | solution.py:140
  51.0 0.1 copy.46
  51.1 0.1 or.25
  51.2 0.1 or.24
  51.3 0.1 sub.76.clone
  51.4 0.1 sub.82
  51.5 0.1 sub.77
  51.7 0.1 concatenate.36
  51.8 0.1 broadcast_in_dim.42
  51.9 0.1 and.192
  52.0 0.1 and.212
  52.1 0.1 and.193
  52.2 0.1 broadcast_in_dim.18
  52.3 0.1 broadcast_in_dim.45
  52.4 0.1 broadcast_in_dim.19
  52.7 0.1 fusion.10
  52.8 0.5 convert_reduce_fusion
  53.3 0.3 select_reduce_fusion
  53.6 0.1 copy.52.idx_ref
  53.7 42.6 %all-to-all-done = bf16[8,128,1024]{2,1,0:T(8,128)(2,1)S(1)} async-done(((bf16[8,128,1024]{2,1,0:T(8,128)(2,1)}), bf16[8,128,1024]{2,1,0:T(8,128)(2,1)S(1)}, u32[]{:S(2)}, u32[]{:S(2)}) %all-to-all-start) | async-done | bytes 2097184 | tf_op jit(solution)/shard_map/all_to_all | solution.py:167
  96.3 43.8 %all-gather.5.cloned.1.call-done.value_hbm = bf16[32768,128]{1,0:T(8,128)(2,1)} async-done(((bf16[1024,128]{1,0:T(8,128)(2,1)}), bf16[32768,128]{1,0:T(8,128)(2,1)}) %all-gather.5.cloned.1.call-update) | async-done | bytes 8388624 | tf_op jit(solution)/shard_map/all_gather | solution.py:171
  140.1 3.4 %copy-done.1 = bf16[32768,128]{1,0:T(8,128)(2,1)S(1)} copy-done((bf16[32768,128]{1,0:T(8,128)(2,1)S(1)}, bf16[32768,128]{1,0:T(8,128)(2,1)}, u32[]{:S(2)}) %copy-start.1) | copy-done | bytes 8388632
  143.5 47.4 %shard_map.55 = bf16[1024,1024]{1,0:T(8,128)(2,1)S(1)} custom-call(s32[128,48]{1,0:T(8,128)S(1)} %copy.52.idx_ref, s32[128]{0:T(128)S(1)} %convert_reduce_fusion.1.count_ref, bf16[1024,1024]{1,0:T(8,128)(2,1)S(1)} %bitcast.50, bf16[32768,128]{1,0:T(8,128)(2,1)S(1)} %copy-done.1, bf16[32768,128]{1,0:T(8,128)(2,1)} %all-gather.5.cloned.1.call-done.value_hbm), custom_call_target="tpu_custom_call" | custom-call | tf_op jit(solution)/shard_map/pallas_call | solution.py:113
  190.9 66.9 %all_to_all.22 = bf16[8,128,1024]{2,1,0:T(8,128)(2,1)S(1)} all-to-all(bf16[8,128,1024]{2,1,0:T(8,128)(2,1)S(1)} %bitcast.51), channel_id=1, replica_groups=mesh['z'=8,'x'=4,'core'=2,'rep'=4] {'z'}, dimensions={0} | all-to-all | bytes 4194304 | tf_op jit(solution)/shard_map/all_to_all | solution.py:176
  257.8 1.6 copy.58
  (29 shorter events, 0.7 us)
Async XLA Ops:
  6.5 1.0 copy-start
  6.5 35.9 %copy-start.2 = (bf16[128,8192]{1,0:T(8,128)(2,1)S(1)}, bf16[128,8192]{1,0:T(8,128)(2,1)}, u32[]{:S(2)}) copy-start(bf16[128,8192]{1,0:T(8,128)(2,1)} %param.5) | copy-start | bytes 6291460
  6.5 89.8 %all-gather.3.cloned.1.call-start = ((), (), s32[]{:S(2)}) async-start(), calls=%async_computation.4 | async-start | bytes 8650752 | tf_op jit(solution)/shard_map/all_gather | solution.py:171
  27.8 112.3 %all-gather.5.cloned.1.call-start = ((), (), s32[]{:S(2)}) async-start(), calls=%async_computation.5 | async-start | bytes 8650752 | tf_op jit(solution)/shard_map/all_gather | solution.py:171
  44.0 3.8 %copy-start.3 = (s32[64,24]{0,1:T(8,128)S(1)}, s32[64,24]{0,1:T(8,128)}, u32[]{:S(2)}) copy-start(s32[64,24]{0,1:T(8,128)} %param.8) | copy-start | bytes 18436
  44.0 3.8 %copy-start.4 = (s32[64,24]{0,1:T(8,128)S(1)}, s32[64,24]{0,1:T(8,128)}, u32[]{:S(2)}) copy-start(s32[64,24]{0,1:T(8,128)} %param.9) | copy-start | bytes 18436
  44.0 52.3 %all-to-all-start = ((bf16[8,128,1024]{2,1,0:T(8,128)(2,1)}), bf16[8,128,1024]{2,1,0:T(8,128)(2,1)S(1)}, u32[]{:S(2)}, u32[]{:S(2)}) async-start(bf16[8,128,1024]{2,1,0:T(8,128)(2,1)} %bitcast.52), calls=%async_computation | async-start | bytes 4194304 | tf_op jit(solution)/shard_map/all_to_all | solution.py:167
  140.1 3.4 %copy-start.1 = (bf16[32768,128]{1,0:T(8,128)(2,1)S(1)}, bf16[32768,128]{1,0:T(8,128)(2,1)}, u32[]{:S(2)}) copy-start(bf16[32768,128]{1,0:T(8,128)(2,1)} %all-gather.3.cloned.1.call-done.key_hbm) | copy-start | bytes 25165828
Sparse Core Ops, SparseCore 0:
  27.9 51.9 all-gather.2
  82.5 57.5 all-gather.4
where the time goes:
time: 270 us; the launch traced here: 266 us
  blocking collectives  101 us (37%)
  waiting for transfers between devices  86.4 us (32%)
  Pallas kernels  47.4 us (18%)
  between operations  13.6 us (5%)
  local copies, waits for them, and re-layouts  10.4 us (4%)
  other arithmetic  3.93 us (1%)
  starting transfers between devices  3.78 us (1%)
    all_to_all x1, blocking collectives, body(): lax.all_to_all(out.reshape(planes, ROWS, HEADS * HEAD_SIZE), 'z', split_a...  66.9 us
    pallas_call x1, Pallas kernels, attend(): pl.pallas_call(functools.partial(attend_kernel, tiles), out_shape=jax.Sha...  47.4 us
    all_gather x2, waiting for transfers between devices, whole(): return lax.all_gather(x, ('rep', 'x', 'core'), axis=0, tiled=True)  43.8 us
    all_to_all x1, waiting for transfers between devices, regroup(): return lax.all_to_all(x, 'z', split_axis=0, concat_axis=0, tiled=True)  42.6 us
    all_to_all x2, blocking collectives, regroup(): return lax.all_to_all(x, 'z', split_axis=0, concat_axis=0, tiled=True)  33.8 us
  transfers between devices with their start and end apart: 3, of which 2 were waited for; matrix products, arithmetic and copies ran while one was open for 3% of the time, Pallas kernels for 0%

commit v1 on v0

v1 whole, which is shorter than its diff:
```python
import functools
import math

import jax
import jax.numpy as jnp
from jax import lax
from jax.experimental import pallas as pl
from jax.experimental.pallas import tpu as pltpu
from jax.sharding import Mesh, PartitionSpec as P

QUERY_HEADS = 64
KEY_VALUE_HEADS = 8
HEADS = QUERY_HEADS // KEY_VALUE_HEADS
HEAD_SIZE = 128
BLOCK = 64
ROWS = 128
SLOTS = 48
TILES = 8
CHUNK = 8
HEAD_CUTS = (0, 4, 8)
NEG_FILL = -1e30
SCALE = math.log2(math.e) / math.sqrt(HEAD_SIZE)


def attend_kernel(
    tiles, first_head, heads, key_at, value_at, idx_ref, count_ref, query_ref, *refs
):
    pieces, refs = refs[: len(key_at) + len(value_at)], refs[len(key_at) + len(value_at) :]
    out_ref, keys, values, scores_a, scores_b, shift_a, shift_b, sem = refs
    score_s, shift_s = (scores_a, scores_b), (shift_a, shift_b)
    width = CHUNK * BLOCK
    slots = iter(range(sem.shape[0]))

    def copies(sources, places, target):
        return [
            pltpu.make_async_copy(
                source.at[pl.ds(a, n), :], target.at[pl.ds(b, n), :], sem.at[next(slots)]
            )
            for source, place in zip(sources, places)
            for a, b, n in place
        ]

    key_copies = copies(pieces[: len(key_at)], key_at, keys)
    value_copies = copies(pieces[len(key_at) :], value_at, values)
    for copy in key_copies + value_copies:
        copy.start()
    for copy in key_copies:
        copy.wait()
    lane = lax.broadcasted_iota(jnp.int32, (1, width), 1)
    wide = lax.broadcasted_iota(jnp.int32, (BLOCK, width), 1)
    causal = (wide >= BLOCK) | (wide <= lax.broadcasted_iota(jnp.int32, (BLOCK, width), 0))
    groups = tiles // TILES
    steps = heads * groups
    every = range(TILES)

    def fold(op, x):
        return functools.reduce(op, [x[:, a : a + 128] for a in range(0, width, 128)])

    def list_of(step, t):
        return (first_head + step // groups) * tiles + (step % groups) * TILES + t

    def place_of(step, t):
        head = step // groups
        return (
            pl.ds(((step % groups) * TILES + t) * BLOCK, BLOCK),
            pl.ds(pl.multiple_of(head * HEAD_SIZE, HEAD_SIZE), HEAD_SIZE),
        )

    def chunks_of(step):
        counts = [count_ref[list_of(step, t)] for t in every]
        return (functools.reduce(jnp.maximum, counts) + CHUNK - 1) // CHUNK

    def gathered(ref, at, c):
        starts = [pl.multiple_of(idx_ref[at, c * CHUNK + j], BLOCK) for j in range(CHUNK)]
        return jnp.concatenate([ref[pl.ds(s, BLOCK), :] for s in starts], axis=0)

    def score(step, side, c, t, best):
        at = list_of(step, t)
        s = lax.dot_general(
            query_ref[place_of(step, t)],
            gathered(keys, at, c),
            (((1,), (1,)), ((), ())),
            preferred_element_type=jnp.float32,
        )
        ok = lane < (count_ref[at] - c * CHUNK) * BLOCK
        if best is None:
            ok = ok & causal
        s = jnp.where(ok, s, NEG_FILL)
        score_s[side][t, c] = s
        top = fold(jnp.maximum, s)
        return top if best is None else jnp.maximum(best, top)

    def mix(step, side, c, t, state):
        shift = jnp.concatenate([shift_s[side][t]] * (width // 128), axis=1)
        p = jnp.exp2(score_s[side][t, c] * SCALE - shift)
        total = fold(jnp.add, p)
        mixed = jnp.dot(
            p.astype(jnp.bfloat16),
            gathered(values, list_of(step, t), c),
            preferred_element_type=jnp.float32,
        )
        return (total, mixed) if state is None else (state[0] + total, state[1] + mixed)

    def settle(side, best):
        for t in every:
            top = jnp.max(best[t], axis=1, keepdims=True) * SCALE
            shift_s[side][t] = jnp.broadcast_to(top, (BLOCK, 128))

    def more_scores(step, side, start, end, best):
        def more(c, best):
            return tuple(score(step, side, c, t, best[t]) for t in every)

        return lax.fori_loop(start, end, more, best)

    best = tuple(score(0, 0, 0, t, None) for t in every)
    settle(0, more_scores(0, 0, 1, chunks_of(0), best))
    for copy in value_copies:
        copy.wait()

    def one_step(step, side):
        other = 1 - side
        later = jnp.minimum(step + 1, steps - 1)
        here = chunks_of(step)
        there = jnp.where(step + 1 < steps, chunks_of(later), 1)
        both = [(mix(step, side, 0, t, None), score(later, other, 0, t, None)) for t in every]

        def fused(c, carried):
            state, best = carried
            both = [
                (mix(step, side, c, t, state[t]), score(later, other, c, t, best[t]))
                for t in every
            ]
            return tuple(x[0] for x in both), tuple(x[1] for x in both)

        shared = jnp.minimum(here, there)
        state, best = lax.fori_loop(
            1, shared, fused, (tuple(x[0] for x in both), tuple(x[1] for x in both))
        )
        state = lax.fori_loop(
            shared, here, lambda c, st: tuple(mix(step, side, c, t, st[t]) for t in every), state
        )
        best = more_scores(later, other, shared, there, best)
        for t in every:
            total, mixed = state[t]
            share = 1.0 / jnp.sum(total, axis=1, keepdims=True)
            out_ref[place_of(step, t)] = (mixed * share).astype(jnp.bfloat16)
        settle(other, best)

    def two_steps(pair, _):
        one_step(2 * pair, 0)
        one_step(2 * pair + 1, 1)
        return 0

    lax.fori_loop(0, steps // 2, two_steps, 0)


def attend(first_head, idx, count, query_rows, key_pieces, value_pieces, key_at, value_at, tokens):
    tiles = query_rows.shape[0] // BLOCK
    heads = query_rows.shape[1] // HEAD_SIZE
    smem = pl.BlockSpec(memory_space=pltpu.SMEM)
    vmem = pl.BlockSpec(memory_space=pltpu.VMEM)
    hbm = pl.BlockSpec(memory_space=pl.ANY)
    return pl.pallas_call(
        functools.partial(attend_kernel, tiles, first_head, heads, key_at, value_at),
        out_shape=jax.ShapeDtypeStruct(query_rows.shape, jnp.bfloat16),
        in_specs=[smem, smem, vmem] + [hbm] * (len(key_pieces) + len(value_pieces)),
        out_specs=vmem,
        scratch_shapes=[
            pltpu.VMEM((tokens, HEAD_SIZE), jnp.bfloat16),
            pltpu.VMEM((tokens, HEAD_SIZE), jnp.bfloat16),
            pltpu.VMEM((TILES, SLOTS // CHUNK, BLOCK, CHUNK * BLOCK), jnp.float32),
            pltpu.VMEM((TILES, SLOTS // CHUNK, BLOCK, CHUNK * BLOCK), jnp.float32),
            pltpu.VMEM((TILES, BLOCK, 128), jnp.float32),
            pltpu.VMEM((TILES, BLOCK, 128), jnp.float32),
            pltpu.SemaphoreType.DMA((sum(len(x) for x in key_at + value_at),)),
        ],
        compiler_params=pltpu.CompilerParams(vmem_limit_bytes=40 << 20),
    )(idx, count, query_rows, *key_pieces, *value_pieces)


def shifted(x, axis, size, by):
    return lax.ppermute(x, axis, [(i, (i + by) % size) for i in range(size)])


def ring_slot(distance, size):
    step = distance % size
    return jnp.where(step == 3, 1, jnp.where(step == 0, 0, step + 1))


def both_ways(xs, axes, beside=()):
    out = [shifted(x, axis, 4, by) for x, axis in zip(xs, axes) for by in (1, -1)]
    out = lax.optimization_barrier(tuple(xs) + tuple(out) + tuple(beside))
    xs, out, beside = out[:2], out[2:6], out[6:]
    return xs, out[::2], out[1::2], beside


def onward(previous, following, axes):
    out = []
    for p, f, axis in zip(previous, following, axes):
        half = p.shape[0] // 2
        out.append(shifted(p[:half], axis, 4, 1))
        out.append(shifted(f[half:], axis, 4, -1))
    return out


def block_lists(vertical, slash, sizes):
    planes, across, cores, reps = sizes
    z, x = lax.axis_index("z"), lax.axis_index("x")
    core, y = lax.axis_index("core"), lax.axis_index("rep")
    per = ROWS // BLOCK
    tiles = planes * per
    columns = lax.dynamic_slice_in_dim(vertical, z * HEADS, HEADS, 0)
    offsets = lax.dynamic_slice_in_dim(slash, z * HEADS, HEADS, 0)
    tile = jnp.arange(tiles, dtype=jnp.int32)
    strip = ((y * planes + tile // per) * across + x) * cores + core
    blocks = strip * per + tile % per
    sources = blocks[None, :, None] - offsets[:, None, :]
    repeated = jnp.any(sources[..., None] == columns[:, None, None, :], axis=-1)
    keep_source = (offsets >= 0)[:, None, :] & (sources >= 0)
    keep_source &= (offsets == 0)[:, None, :] | ~repeated
    spread = jnp.broadcast_to(columns[:, None, :], sources.shape)
    keep_column = (spread >= 0) & (spread < blocks[None, :, None])
    picks = jnp.concatenate([sources, spread], axis=-1).reshape(HEADS * tiles, SLOTS)
    keep = jnp.concatenate([keep_source, keep_column], axis=-1).reshape(HEADS * tiles, SLOTS)
    slot = jnp.arange(SLOTS, dtype=jnp.int32)
    place = jnp.sum((keep[:, None, :] & (slot[None, :] < slot[:, None])[None]).astype(jnp.int32), -1)
    half = picks % per
    strip = picks // per
    core_of = (strip + core) % cores
    x_of = ring_slot(strip // cores - x, across)
    z_of = strip // (cores * across) % planes
    y_of = ring_slot(strip // (cores * across * planes) - y, reps)
    where = ((((core_of * reps + y_of) * across + x_of) * planes + z_of) * per + half) * BLOCK
    hit = keep[:, None, :] & (place[:, None, :] == slot[None, :, None])
    idx = jnp.sum(jnp.where(hit, where[:, None, :], 0), axis=-1)
    return idx, jnp.sum(keep.astype(jnp.int32), axis=-1)


def body(sizes, queries, keys, values, vertical, slash):
    planes, across, cores, reps = sizes
    idx, count = block_lists(vertical, slash, sizes)

    def regroup(x):
        return lax.all_to_all(x, "z", split_axis=0, concat_axis=0, tiled=True)

    def by_plane(x):
        return x.reshape(ROWS, planes, -1).transpose(1, 0, 2)

    pair = regroup(jnp.concatenate([by_plane(keys), by_plane(values)], axis=1))
    own = planes * ROWS
    key_rows = pair[:, :ROWS].reshape(own, HEAD_SIZE)
    value_rows = pair[:, ROWS:].reshape(own, HEAD_SIZE)
    axes = ("x", "rep")
    xs, previous, following, _ = both_ways((key_rows, value_rows), axes)
    far = lax.optimization_barrier(tuple(onward(previous, following, axes)))
    xs = [
        jnp.concatenate([xs[i], previous[i], following[i], far[2 * i], far[2 * i + 1]], axis=0)
        for i in range(2)
    ]
    axes = ("rep", "x")
    *xs, queries = lax.optimization_barrier((*xs, queries))
    query_rows = regroup(by_plane(queries)).reshape(own, HEADS * HEAD_SIZE)
    cuts = [a * HEAD_SIZE for a in HEAD_CUTS]
    query_parts = [query_rows[:, a:b] for a, b in zip(cuts, cuts[1:])]
    beside = (idx, count, *[shifted(x, "core", cores, 1) for x in xs])
    xs, previous, following, beside = both_ways(xs, axes, beside)
    idx, count, *across_core = beside
    far = onward(previous, following, axes)
    pieces = []
    for i in range(2):
        near = [xs[i], previous[i], following[i]]
        other = [across_core[i]] + [shifted(p, "core", cores, 1) for p in near[1:]]
        pieces.append((near + far[2 * i : 2 * i + 2], other))
    far = lax.optimization_barrier(tuple(far))
    for i in range(2):
        last = [shifted(p, "core", cores, 1) for p in far[2 * i : 2 * i + 2]]
        pieces[i] = pieces[i][0] + pieces[i][1] + last
    key_pieces, value_pieces = pieces

    key_at, value_at = [], []
    place = 0
    for piece in key_pieces:
        key_at.append([(0, place, piece.shape[0])])
        place += piece.shape[0]
    place = 0
    for piece in value_pieces:
        parts = []
        for a in range(0, piece.shape[0], own):
            core_of, rest = divmod((place + a) // own, across * reps)
            x_of, y_of = divmod(rest, reps)
            parts.append((a, ((core_of * reps + y_of) * across + x_of) * own, own))
        value_at.append(parts)
        place += piece.shape[0]

    outs = []
    first_head = 0
    for query_rows in query_parts:
        out = attend(
            first_head, idx, count, query_rows, key_pieces, value_pieces, key_at, value_at, place
        )
        first_head += query_rows.shape[1] // HEAD_SIZE
        outs.append(regroup(out.reshape(planes, ROWS, query_rows.shape[1])))
    out = jnp.concatenate(outs, axis=2)
    return out.transpose(1, 0, 2).reshape(ROWS, QUERY_HEADS * HEAD_SIZE)


def solution(mesh):
    reps = mesh.devices.shape[1]
    sizes = (8, 4, 2, reps)
    split = Mesh(mesh.devices.reshape(sizes), ("z", "x", "core", "rep"))
    rows = P(("rep", "z", "x", "core"), None)
    return jax.shard_map(
        functools.partial(body, sizes),
        mesh=split,
        in_specs=(rows, rows, rows, P(), P()),
        out_specs=rows,
        check_vma=False,
    )
```

time: 270 us -> 237 us (0.88); the launches traced: 266 us -> 237 us
  waiting for transfers between devices: 86.4 us -> 40.3 us
  blocking collectives: 101 us -> 58.1 us
  starting transfers between devices: 3.78 us -> 36.4 us
  local copies, waits for them, and re-layouts: 10.4 us -> 30.9 us
  Pallas kernels: 47.4 us -> 65.3 us
  between operations: 13.6 us -> 0.48 us
    all_to_all x1 -> x0, blocking collectives: 66.9 us -> none  [body(): lax.all_to_all(out.reshape(planes, ROWS, HEADS * HEAD_SIZE), 'z', split_a...]
    all_gather x2 -> x0, waiting for transfers between devices: 43.8 us -> none  [whole(): return lax.all_gather(x, ('rep', 'x', 'core'), axis=0, tiled=True)]
    all_to_all x1 -> x2, waiting for transfers between devices: 42.6 us -> 0.01 us  [regroup(): return lax.all_to_all(x, 'z', split_axis=0, concat_axis=0, tiled=True)]
    ppermute x0 -> x26, waiting for transfers between devices: none -> 40.2 us  [shifted(): return lax.ppermute(x, axis, [(i, (i + by) % size) for i in range(size)])]
    all_to_all x2, blocking collectives: 33.8 us -> 58.1 us  [regroup(): return lax.all_to_all(x, 'z', split_axis=0, concat_axis=0, tiled=True)]
    ppermute x0 -> x26, starting transfers between devices: none -> 19.3 us  [shifted(): return lax.ppermute(x, axis, [(i, (i + by) % size) for i in range(size)])]
    pallas_call x1 -> x2, Pallas kernels: 47.4 us -> 65.3 us  [attend(): pl.pallas_call(functools.partial(attend_kernel, tiles, first_head, heads,...]
    all_to_all x1 -> x2, starting transfers between devices: 3.74 us -> 17.1 us  [regroup(): return lax.all_to_all(x, 'z', split_axis=0, concat_axis=0, tiled=True)]
  transfers between devices with their start and end apart: 3 -> 28, of which waited for: 2 -> 13; matrix products, arithmetic and copies ran while one was open for 3% -> 7% of each run, Pallas kernels for 0% -> 15%
where the time goes in v1:
time: 237 us
  Pallas kernels  65.3 us (28%)
  blocking collectives  58.1 us (25%)
  waiting for transfers between devices  40.3 us (17%)
  starting transfers between devices  36.4 us (15%)
  local copies, waits for them, and re-layouts  30.9 us (13%)
  other arithmetic  5.44 us (2%)
    pallas_call x2, Pallas kernels, attend(): pl.pallas_call(functools.partial(attend_kernel, tiles, first_head, heads,...  65.3 us
    all_to_all x2, blocking collectives, regroup(): return lax.all_to_all(x, 'z', split_axis=0, concat_axis=0, tiled=True)  58.1 us
    ppermute x26, waiting for transfers between devices, shifted(): return lax.ppermute(x, axis, [(i, (i + by) % size) for i in range(size)])  40.2 us
    ppermute x26, starting transfers between devices, shifted(): return lax.ppermute(x, axis, [(i, (i + by) % size) for i in range(size)])  19.3 us
    unnamed x50, local copies, waits for them, and re-layouts  17.5 us
    all_to_all x2, starting transfers between devices, regroup(): return lax.all_to_all(x, 'z', split_axis=0, concat_axis=0, tiled=True)  17.1 us
  transfers between devices with their start and end apart: 28, of which 13 were waited for; matrix products, arithmetic and copies ran while one was open for 7% of the time, Pallas kernels for 15%

profile of v1, /device:TPU:30, one launch (start us, length us, event | category | flops | bytes accessed | tf_op | source)
XLA Modules:
  0.0 236.9 jit_solution(16577720406788533278)
XLA Ops:
  2.1 25.8 %all_to_all.20 = bf16[8,256,128]{2,1,0:T(8,128)(2,1)S(1)} all-to-all(bf16[8,256,128]{2,1,0:T(8,128)(2,1)S(1)} %pad_maximum_fusion), channel_id=1, replica_groups=mesh['z'=8,'x'=4,'core'=2,'rep'=4] {'z'}, dimensions={0} | all-to-all | bytes 1048576 | tf_op jit(solution)/shard_map/all_to_all | solution.py:244
  28.4 1.5 collective-permute-start.1
  30.2 1.8 collective-permute-start.3
  32.0 2.3 collective-permute-done
  34.3 1.7 collective-permute-done.1
  36.4 1.4 collective-permute-done.3
  38.0 1.8 collective-permute-start.4
  40.5 1.7 collective-permute-start.7
  44.4 1.5 collective-permute-done.5
  48.6 3.2 %copy.64 = bf16[16,8,8,1024]{3,2,0,1:T(8,128)(2,1)} copy(bf16[16,8,8,1024]{3,2,1,0:T(8,128)(2,1)} %bitcast.55) | data formatting | bytes 4194304 | tf_op jit(solution)/shard_map/reshape | solution.py:247
  51.8 4.4 %all-to-all-start.1 = ((bf16[8,128,1024]{2,1,0:T(8,128)(2,1)}), bf16[8,128,1024]{2,1,0:T(8,128)(2,1)}, u32[]{:S(2)}, u32[]{:S(2)}) async-start(bf16[8,128,1024]{2,1,0:T(8,128)(2,1)} %bitcast.54), calls=%async_computation.1 | async-start | bytes 4194304 | tf_op jit(solution)/shard_map/all_to_all | solution.py:244
  56.4 2.8 %compare_reduce_fusion = pred[8,16,24]{2,1,0:T(8,128)(4,1)S(1)} fusion(s32[8,24]{1,0:T(8,128)S(1)} %copy.48, s32[8,16,24]{2,1,0:T(8,128)S(1)} %broadcast_subtract_fusion), kind=kLoop, calls=%fused_computation.2 | loop fusion | flops 144384 | bytes 16128 | tf_op jit(solution)/shard_map/reduce_or | solution.py:218
  60.9 1.7 collective-permute-start.9
  62.6 2.9 %collective-permute-start.10 = (bf16[4096,128]{1,0:T(8,128)(2,1)}, bf16[4096,128]{1,0:T(8,128)(2,1)}, u32[]{:S(2)}, u32[]{:S(2)}) collective-permute-start(bf16[4096,128]{1,0:T(8,128)(2,1)} %constant_dynamic-update-slice_fusion.5.refs_10_), channel_id=1, source_target_pairs={{0,8},{8,16},{16,24},{24,0},{1,9},{9,17},{17,25},{25,1},{2,10},{10... | collective-permute-start | bytes 3145736 | tf_op jit(solution)/shard_map/ppermute | solution.py:182
  65.5 2.1 collective-permute-done.8.refs_1_
  68.6 12.7 %collective-permute-done.9.refs_2_ = bf16[4096,128]{1,0:T(8,128)(2,1)S(1)} collective-permute-done((bf16[4096,128]{1,0:T(8,128)(2,1)S(1)}, bf16[4096,128]{1,0:T(8,128)(2,1)S(1)}, u32[]{:S(2)}, u32[]{:S(2)}) %collective-permute-start.9) | collective-permute-done | bytes 1048608 | tf_op jit(solution)/shard_map/ppermute | solution.py:182
  82.2 3.4 %collective-permute-done.11.refs_12_ = bf16[4096,128]{1,0:T(8,128)(2,1)} collective-permute-done((bf16[4096,128]{1,0:T(8,128)(2,1)}, bf16[4096,128]{1,0:T(8,128)(2,1)}, u32[]{:S(2)}, u32[]{:S(2)}) %collective-permute-start.11) | collective-permute-done | bytes 1048608 | tf_op jit(solution)/shard_map/ppermute | solution.py:182
  86.7 1.9 collective-permute-start.14
  91.5 1.8 collective-permute-start.19
  93.3 2.7 %collective-permute-done.14.refs_3_ = bf16[2048,128]{1,0:T(8,128)(2,1)S(1)} collective-permute-done((bf16[2048,128]{1,0:T(8,128)(2,1)S(1)}, bf16[2048,128]{1,0:T(8,128)(2,1)S(1)}, u32[]{:S(2)}, u32[]{:S(2)}) %collective-permute-start.14) | collective-permute-done | bytes 524320 | tf_op jit(solution)/shard_map/ppermute | solution.py:182
  96.0 8.5 %collective-permute-done.15.refs_4_ = bf16[2048,128]{1,0:T(8,128)(2,1)} collective-permute-done((bf16[2048,128]{1,0:T(8,128)(2,1)S(1)}, bf16[2048,128]{1,0:T(8,128)(2,1)}, u32[]{:S(2)}, u32[]{:S(2)}) %collective-permute-start.15) | collective-permute-done | bytes 524320 | tf_op jit(solution)/shard_map/ppermute | solution.py:182
  104.9 1.8 collective-permute-done.19.refs_14_
  111.6 2.8 %fusion.33 = (bf16[1024,512]{1,0:T(8,128)(2,1)}, bf16[1024,512]{1,0:T(8,128)(2,1)S(1)}) fusion(bf16[1024,1024]{1,0:T(8,128)(2,1)} %bitcast.6), kind=kLoop, calls=%fused_computation.102 | loop fusion | bytes 4194304 | tf_op jit(solution)/shard_map/slice | solution.py:264
  114.5 28.6 %shard_map.56 = bf16[1024,512]{1,0:T(8,128)(2,1)S(1)} custom-call(s32[128,48]{1,0:T(8,128)S(1)} %copy.53.idx_ref, s32[128]{0:T(128)S(1)} %convert_reduce_fusion.1.count_ref, bf16[1024,512]{1,0:T(8,128)(2,1)S(1)} %get-tuple-element.66.query_ref, bf16[4096,128]{1,0:T(8,128)(2,1)S(1)} %constant_dynamic-update-slice_fusion.refs_0_, ...), custom_call_target="tpu_custom_call" | custom-call | tf_op jit(solution)/shard_map/pallas_call | solution.py:163
  144.1 12.8 %all-to-all-start.3 = ((bf16[8,128,512]{2,1,0:T(8,128)(2,1)}), bf16[8,128,512]{2,1,0:T(8,128)(2,1)}, u32[]{:S(2)}, u32[]{:S(2)}) async-start(bf16[8,128,512]{2,1,0:T(8,128)(2,1)} %bitcast.52), calls=%async_computation.3 | async-start | bytes 2097152 | tf_op jit(solution)/shard_map/all_to_all | solution.py:244
  158.0 1.2 copy-done.6
  159.3 1.2 copy-done.9
  160.5 1.2 copy-done.12
  163.8 36.7 %shard_map.55 = bf16[1024,512]{1,0:T(8,128)(2,1)S(1)} custom-call(s32[128,48]{1,0:T(8,128)S(1)} %copy.53.idx_ref, s32[128]{0:T(128)S(1)} %convert_reduce_fusion.1.count_ref, bf16[1024,512]{1,0:T(8,128)(2,1)S(1)} %copy-done.12, bf16[4096,128]{1,0:T(8,128)(2,1)S(1)} %constant_dynamic-update-slice_fusion.refs_0_, ...), custom_call_target="tpu_custom_call" | custom-call | tf_op jit(solution)/shard_map/pallas_call | solution.py:163
  201.5 32.4 %all_to_all.21 = bf16[8,128,512]{2,1,0:T(8,128)(2,1)S(1)} all-to-all(bf16[8,128,512]{2,1,0:T(8,128)(2,1)} %bitcast.53), channel_id=1, replica_groups=mesh['z'=8,'x'=4,'core'=2,'rep'=4] {'z'}, dimensions={0} | all-to-all | bytes 2097152 | tf_op jit(solution)/shard_map/all_to_all | solution.py:244
  233.8 1.5 maximum_bitcast_fusion
  235.3 1.6 copy.60
  (130 shorter events, 27.1 us)
Async XLA Ops:
  27.9 6.4 %collective-permute-start = (bf16[1024,128]{1,0:T(8,128)(2,1)S(1)}, bf16[1024,128]{1,0:T(8,128)(2,1)S(1)}, u32[]{:S(2)}, u32[]{:S(2)}) collective-permute-start(bf16[1024,128]{1,0:T(8,128)(2,1)S(1)} %bitcast.59), channel_id=1, source_target_pairs={{0,8},{8,16},{16,24},{24,0},{1,9},{9,17},{17,25},{25,1},{2,10},{10... | collective-permute-start | bytes 786440 | tf_op jit(solution)/shard_map/ppermute | solution.py:182
  28.4 7.6 %collective-permute-start.1 = (bf16[1024,128]{1,0:T(8,128)(2,1)S(1)}, bf16[1024,128]{1,0:T(8,128)(2,1)S(1)}, u32[]{:S(2)}, u32[]{:S(2)}) collective-permute-start(bf16[1024,128]{1,0:T(8,128)(2,1)S(1)} %bitcast.60), channel_id=1, source_target_pairs={{0,24},{8,0},{16,8},{24,16},{1,25},{9,1},{17,9},{25,17},{2,26},{10... | collective-permute-start | bytes 786440 | tf_op jit(solution)/shard_map/ppermute | solution.py:182
  30.0 6.4 %collective-permute-start.2 = (bf16[1024,128]{1,0:T(8,128)(2,1)S(1)}, bf16[1024,128]{1,0:T(8,128)(2,1)S(1)}, u32[]{:S(2)}, u32[]{:S(2)}) collective-permute-start(bf16[1024,128]{1,0:T(8,128)(2,1)S(1)} %bitcast.56), channel_id=1, source_target_pairs={{0,1},{1,2},{2,3},{3,0},{4,5},{5,6},{6,7},{7,4},{8,9},{9,10},{10,1... | collective-permute-start | bytes 786440 | tf_op jit(solution)/shard_map/ppermute | solution.py:182
  30.2 7.6 %collective-permute-start.3 = (bf16[1024,128]{1,0:T(8,128)(2,1)S(1)}, bf16[1024,128]{1,0:T(8,128)(2,1)S(1)}, u32[]{:S(2)}, u32[]{:S(2)}) collective-permute-start(bf16[1024,128]{1,0:T(8,128)(2,1)S(1)} %bitcast.57), channel_id=1, source_target_pairs={{0,3},{1,0},{2,1},{3,2},{4,7},{5,4},{6,5},{7,6},{8,11},{9,8},{10,9... | collective-permute-start | bytes 786440 | tf_op jit(solution)/shard_map/ppermute | solution.py:182
  37.9 10.7 %copy-start.19 = (s32[64,24]{0,1:T(8,128)S(1)}, s32[64,24]{0,1:T(8,128)}, u32[]{:S(2)}) copy-start(s32[64,24]{0,1:T(8,128)} %param.8) | copy-start | bytes 18436
  37.9 10.6 %copy-start.20 = (s32[64,24]{0,1:T(8,128)S(1)}, s32[64,24]{0,1:T(8,128)}, u32[]{:S(2)}) copy-start(s32[64,24]{0,1:T(8,128)} %param.9) | copy-start | bytes 18436
  38.0 6.5 %collective-permute-start.4 = (bf16[512,128]{1,0:T(8,128)(2,1)S(1)}, bf16[512,128]{1,0:T(8,128)(2,1)S(1)}, u32[]{:S(2)}, u32[]{:S(2)}) collective-permute-start(bf16[512,128]{1,0:T(8,128)(2,1)S(1)} %slice.38), channel_id=1, source_target_pairs={{0,8},{8,16},{16,24},{24,0},{1,9},{9,17},{17,25},{25,1},{2,10},{10... | collective-permute-start | bytes 393224 | tf_op jit(solution)/shard_map/ppermute | solution.py:182
  39.7 6.2 %collective-permute-start.5 = (bf16[512,128]{1,0:T(8,128)(2,1)S(1)}, bf16[512,128]{1,0:T(8,128)(2,1)S(1)}, u32[]{:S(2)}, u32[]{:S(2)}) collective-permute-start(bf16[512,128]{1,0:T(8,128)(2,1)S(1)} %slice.39), channel_id=1, source_target_pairs={{0,24},{8,0},{16,8},{24,16},{1,25},{9,1},{17,9},{25,17},{2,26},{10... | collective-permute-start | bytes 393224 | tf_op jit(solution)/shard_map/ppermute | solution.py:182
  40.1 5.8 %collective-permute-start.6 = (bf16[512,128]{1,0:T(8,128)(2,1)S(1)}, bf16[512,128]{1,0:T(8,128)(2,1)S(1)}, u32[]{:S(2)}, u32[]{:S(2)}) collective-permute-start(bf16[512,128]{1,0:T(8,128)(2,1)S(1)} %slice.40), channel_id=1, source_target_pairs={{0,1},{1,2},{2,3},{3,0},{4,5},{5,6},{6,7},{7,4},{8,9},{9,10},{10,1... | collective-permute-start | bytes 393224 | tf_op jit(solution)/shard_map/ppermute | solution.py:182
  40.5 6.3 %collective-permute-start.7 = (bf16[512,128]{1,0:T(8,128)(2,1)S(1)}, bf16[512,128]{1,0:T(8,128)(2,1)S(1)}, u32[]{:S(2)}, u32[]{:S(2)}) collective-permute-start(bf16[512,128]{1,0:T(8,128)(2,1)S(1)} %slice.41), channel_id=1, source_target_pairs={{0,3},{1,0},{2,1},{3,2},{4,7},{5,4},{6,5},{7,6},{8,11},{9,8},{10,9... | collective-permute-start | bytes 393224 | tf_op jit(solution)/shard_map/ppermute | solution.py:182
  48.2 19.4 %collective-permute-start.8 = (bf16[4096,128]{1,0:T(8,128)(2,1)S(1)}, bf16[4096,128]{1,0:T(8,128)(2,1)S(1)}, u32[]{:S(2)}, u32[]{:S(2)}) collective-permute-start(bf16[4096,128]{1,0:T(8,128)(2,1)S(1)} %constant_dynamic-update-slice_fusion.refs_0_), channel_id=1, source_target_pairs={{0,1},{1,2},{2,3},{3,0},{4,5},{5,6},{6,7},{7,4},{8,9},{9,10},{10,1... | collective-permute-start | bytes 3145736 | tf_op jit(solution)/shard_map/ppermute | solution.py:182
  51.8 59.8 %all-to-all-start.1 = ((bf16[8,128,1024]{2,1,0:T(8,128)(2,1)}), bf16[8,128,1024]{2,1,0:T(8,128)(2,1)}, u32[]{:S(2)}, u32[]{:S(2)}) async-start(bf16[8,128,1024]{2,1,0:T(8,128)(2,1)} %bitcast.54), calls=%async_computation.1 | async-start | bytes 4194304 | tf_op jit(solution)/shard_map/all_to_all | solution.py:244
  60.9 20.4 %collective-permute-start.9 = (bf16[4096,128]{1,0:T(8,128)(2,1)S(1)}, bf16[4096,128]{1,0:T(8,128)(2,1)S(1)}, u32[]{:S(2)}, u32[]{:S(2)}) collective-permute-start(bf16[4096,128]{1,0:T(8,128)(2,1)S(1)} %constant_dynamic-update-slice_fusion.refs_0_), channel_id=1, source_target_pairs={{0,3},{1,0},{2,1},{3,2},{4,7},{5,4},{6,5},{7,6},{8,11},{9,8},{10,9... | collective-permute-start | bytes 3145736 | tf_op jit(solution)/shard_map/ppermute | solution.py:182
  62.6 19.6 %collective-permute-start.10 = (bf16[4096,128]{1,0:T(8,128)(2,1)}, bf16[4096,128]{1,0:T(8,128)(2,1)}, u32[]{:S(2)}, u32[]{:S(2)}) collective-permute-start(bf16[4096,128]{1,0:T(8,128)(2,1)} %constant_dynamic-update-slice_fusion.5.refs_10_), channel_id=1, source_target_pairs={{0,8},{8,16},{16,24},{24,0},{1,9},{9,17},{17,25},{25,1},{2,10},{10... | collective-permute-start | bytes 3145736 | tf_op jit(solution)/shard_map/ppermute | solution.py:182
  65.5 20.1 %collective-permute-start.11 = (bf16[4096,128]{1,0:T(8,128)(2,1)}, bf16[4096,128]{1,0:T(8,128)(2,1)}, u32[]{:S(2)}, u32[]{:S(2)}) collective-permute-start(bf16[4096,128]{1,0:T(8,128)(2,1)} %constant_dynamic-update-slice_fusion.5.refs_10_), channel_id=1, source_target_pairs={{0,24},{8,0},{16,8},{24,16},{1,25},{9,1},{17,9},{25,17},{2,26},{10... | collective-permute-start | bytes 3145736 | tf_op jit(solution)/shard_map/ppermute | solution.py:182
  65.5 20.1 %collective-permute-start.12 = (bf16[4096,128]{1,0:T(8,128)(2,1)S(1)}, bf16[4096,128]{1,0:T(8,128)(2,1)S(1)}, u32[]{:S(2)}, u32[]{:S(2)}) collective-permute-start(bf16[4096,128]{1,0:T(8,128)(2,1)S(1)} %constant_dynamic-update-slice_fusion.refs_0_), channel_id=1, source_target_pairs={{0,4},{4,0},{1,5},{5,1},{2,6},{6,2},{3,7},{7,3},{8,12},{12,8},{9,1... | collective-permute-start | bytes 3145736 | tf_op jit(solution)/shard_map/ppermute | solution.py:182
  67.6 19.1 %collective-permute-start.13 = (bf16[4096,128]{1,0:T(8,128)(2,1)}, bf16[4096,128]{1,0:T(8,128)(2,1)}, u32[]{:S(2)}, u32[]{:S(2)}) collective-permute-start(bf16[4096,128]{1,0:T(8,128)(2,1)} %constant_dynamic-update-slice_fusion.5.refs_10_), channel_id=1, source_target_pairs={{0,4},{4,0},{1,5},{5,1},{2,6},{6,2},{3,7},{7,3},{8,12},{12,8},{9,1... | collective-permute-start | bytes 3145736 | tf_op jit(solution)/shard_map/ppermute | solution.py:182
  86.7 9.3 %collective-permute-start.14 = (bf16[2048,128]{1,0:T(8,128)(2,1)S(1)}, bf16[2048,128]{1,0:T(8,128)(2,1)S(1)}, u32[]{:S(2)}, u32[]{:S(2)}) collective-permute-start(bf16[2048,128]{1,0:T(8,128)(2,1)S(1)} %slice.43), channel_id=1, source_target_pairs={{0,1},{1,2},{2,3},{3,0},{4,5},{5,6},{6,7},{7,4},{8,9},{9,10},{10,1... | collective-permute-start | bytes 1572872 | tf_op jit(solution)/shard_map/ppermute | solution.py:182
  88.7 18.9 %collective-permute-start.16 = (bf16[4096,128]{1,0:T(8,128)(2,1)S(1)}, bf16[4096,128]{1,0:T(8,128)(2,1)S(1)}, u32[]{:S(2)}, u32[]{:S(2)}) collective-permute-start(bf16[4096,128]{1,0:T(8,128)(2,1)S(1)} %collective-permute-done.8.refs_1_), channel_id=1, source_target_pairs={{0,4},{4,0},{1,5},{5,1},{2,6},{6,2},{3,7},{7,3},{8,12},{12,8},{9,1... | collective-permute-start | bytes 3145736 | tf_op jit(solution)/shard_map/ppermute | solution.py:182
  88.7 15.7 %collective-permute-start.15 = (bf16[2048,128]{1,0:T(8,128)(2,1)S(1)}, bf16[2048,128]{1,0:T(8,128)(2,1)}, u32[]{:S(2)}, u32[]{:S(2)}) collective-permute-start(bf16[2048,128]{1,0:T(8,128)(2,1)S(1)} %slice.44), channel_id=1, source_target_pairs={{0,3},{1,0},{2,1},{3,2},{4,7},{5,4},{6,5},{7,6},{8,11},{9,8},{10,9... | collective-permute-start | bytes 1572872 | tf_op jit(solution)/shard_map/ppermute | solution.py:182
  90.0 14.4 %collective-permute-start.18 = (bf16[2048,128]{1,0:T(8,128)(2,1)S(1)}, bf16[2048,128]{1,0:T(8,128)(2,1)}, u32[]{:S(2)}, u32[]{:S(2)}) collective-permute-start(bf16[2048,128]{1,0:T(8,128)(2,1)S(1)} %slice.45), channel_id=1, source_target_pairs={{0,8},{8,16},{16,24},{24,0},{1,9},{9,17},{17,25},{25,1},{2,10},{10... | collective-permute-start | bytes 1572872 | tf_op jit(solution)/shard_map/ppermute | solution.py:182
  91.5 15.3 %collective-permute-start.19 = (bf16[2048,128]{1,0:T(8,128)(2,1)S(1)}, bf16[2048,128]{1,0:T(8,128)(2,1)}, u32[]{:S(2)}, u32[]{:S(2)}) collective-permute-start(bf16[2048,128]{1,0:T(8,128)(2,1)S(1)} %slice.46), channel_id=1, source_target_pairs={{0,24},{8,0},{16,8},{24,16},{1,25},{9,1},{17,9},{25,17},{2,26},{10... | collective-permute-start | bytes 1572872 | tf_op jit(solution)/shard_map/ppermute | solution.py:182
  96.0 13.1 %collective-permute-start.17 = (bf16[4096,128]{1,0:T(8,128)(2,1)S(1)}, bf16[4096,128]{1,0:T(8,128)(2,1)S(1)}, u32[]{:S(2)}, u32[]{:S(2)}) collective-permute-start(bf16[4096,128]{1,0:T(8,128)(2,1)S(1)} %collective-permute-done.9.refs_2_), channel_id=1, source_target_pairs={{0,4},{4,0},{1,5},{5,1},{2,6},{6,2},{3,7},{7,3},{8,12},{12,8},{9,1... | collective-permute-start | bytes 3145736 | tf_op jit(solution)/shard_map/ppermute | solution.py:182
  104.4 9.9 %collective-permute-start.22 = (bf16[4096,128]{1,0:T(8,128)(2,1)}, bf16[4096,128]{1,0:T(8,128)(2,1)}, u32[]{:S(2)}, u32[]{:S(2)}) collective-permute-start(bf16[4096,128]{1,0:T(8,128)(2,1)} %collective-permute-done.10.refs_11_), channel_id=1, source_target_pairs={{0,4},{4,0},{1,5},{5,1},{2,6},{6,2},{3,7},{7,3},{8,12},{12,8},{9,1... | collective-permute-start | bytes 3145736 | tf_op jit(solution)/shard_map/ppermute | solution.py:182
  104.4 9.9 %collective-permute-start.23 = (bf16[4096,128]{1,0:T(8,128)(2,1)}, bf16[4096,128]{1,0:T(8,128)(2,1)}, u32[]{:S(2)}, u32[]{:S(2)}) collective-permute-start(bf16[4096,128]{1,0:T(8,128)(2,1)} %collective-permute-done.11.refs_12_), channel_id=1, source_target_pairs={{0,4},{4,0},{1,5},{5,1},{2,6},{6,2},{3,7},{7,3},{8,12},{12,8},{9,1... | collective-permute-start | bytes 3145736 | tf_op jit(solution)/shard_map/ppermute | solution.py:182
  106.8 3.3 %collective-permute-start.20 = (bf16[2048,128]{1,0:T(8,128)(2,1)S(1)}, bf16[2048,128]{1,0:T(8,128)(2,1)S(1)}, u32[]{:S(2)}, u32[]{:S(2)}) collective-permute-start(bf16[2048,128]{1,0:T(8,128)(2,1)S(1)} %collective-permute-done.14.refs_3_), channel_id=1, source_target_pairs={{0,4},{4,0},{1,5},{5,1},{2,6},{6,2},{3,7},{7,3},{8,12},{12,8},{9,1... | collective-permute-start | bytes 1572872 | tf_op jit(solution)/shard_map/ppermute | solution.py:182
  108.6 5.8 %collective-permute-start.21 = (bf16[2048,128]{1,0:T(8,128)(2,1)}, bf16[2048,128]{1,0:T(8,128)(2,1)}, u32[]{:S(2)}, u32[]{:S(2)}) collective-permute-start(bf16[2048,128]{1,0:T(8,128)(2,1)} %collective-permute-done.15.refs_4_), channel_id=1, source_target_pairs={{0,4},{4,0},{1,5},{5,1},{2,6},{6,2},{3,7},{7,3},{8,12},{12,8},{9,1... | collective-permute-start | bytes 1572872 | tf_op jit(solution)/shard_map/ppermute | solution.py:182
  110.1 4.3 %collective-permute-start.24 = (bf16[2048,128]{1,0:T(8,128)(2,1)}, bf16[2048,128]{1,0:T(8,128)(2,1)}, u32[]{:S(2)}, u32[]{:S(2)}) collective-permute-start(bf16[2048,128]{1,0:T(8,128)(2,1)} %collective-permute-done.18.refs_13_), channel_id=1, source_target_pairs={{0,4},{4,0},{1,5},{5,1},{2,6},{6,2},{3,7},{7,3},{8,12},{12,8},{9,1... | collective-permute-start | bytes 1572872 | tf_op jit(solution)/shard_map/ppermute | solution.py:182
  110.9 3.5 %collective-permute-start.25 = (bf16[2048,128]{1,0:T(8,128)(2,1)}, bf16[2048,128]{1,0:T(8,128)(2,1)}, u32[]{:S(2)}, u32[]{:S(2)}) collective-permute-start(bf16[2048,128]{1,0:T(8,128)(2,1)} %collective-permute-done.19.refs_14_), channel_id=1, source_target_pairs={{0,4},{4,0},{1,5},{5,1},{2,6},{6,2},{3,7},{7,3},{8,12},{12,8},{9,1... | collective-permute-start | bytes 1572872 | tf_op jit(solution)/shard_map/ppermute | solution.py:182
  111.5 2.9 %copy-start.2 = (bf16[4096,128]{1,0:T(8,128)(2,1)S(1)}, bf16[4096,128]{1,0:T(8,128)(2,1)}, u32[]{:S(2)}) copy-start(bf16[4096,128]{1,0:T(8,128)(2,1)} %copy-done.1) | copy-start | bytes 3145732
  111.5 2.9 %copy-start.5 = (bf16[4096,128]{1,0:T(8,128)(2,1)S(1)}, bf16[4096,128]{1,0:T(8,128)(2,1)}, u32[]{:S(2)}) copy-start(bf16[4096,128]{1,0:T(8,128)(2,1)} %copy-done.4) | copy-start | bytes 3145732
  144.1 57.4 %all-to-all-start.3 = ((bf16[8,128,512]{2,1,0:T(8,128)(2,1)}), bf16[8,128,512]{2,1,0:T(8,128)(2,1)}, u32[]{:S(2)}, u32[]{:S(2)}) async-start(bf16[8,128,512]{2,1,0:T(8,128)(2,1)} %bitcast.52), calls=%async_computation.3 | async-start | bytes 2097152 | tf_op jit(solution)/shard_map/all_to_all | solution.py:244
  (17 other events, 23.2 us)

commit v2 on v1

--- a/solution.py
+++ b/solution.py
@@ -67,7 +67,7 @@
         )
 
     def chunks_of(step):
-        counts = [count_ref[list_of(step, t)] for t in every]
+        counts = [count_ref[list_of(step, t), 0] for t in every]
         return (functools.reduce(jnp.maximum, counts) + CHUNK - 1) // CHUNK
 
     def gathered(ref, at, c):
@@ -82,7 +82,7 @@
             (((1,), (1,)), ((), ())),
             preferred_element_type=jnp.float32,
         )
-        ok = lane < (count_ref[at] - c * CHUNK) * BLOCK
+        ok = lane < (count_ref[at, 0] - c * CHUNK) * BLOCK
         if best is None:
             ok = ok & causal
         s = jnp.where(ok, s, NEG_FILL)
@@ -203,37 +203,72 @@
     return out
 
 
-def block_lists(vertical, slash, sizes):
+def list_kernel(sizes, vertical_s, vertical_ref, slash_ref, idx_ref, count_ref):
     planes, across, cores, reps = sizes
     z, x = lax.axis_index("z"), lax.axis_index("x")
     core, y = lax.axis_index("core"), lax.axis_index("rep")
     per = ROWS // BLOCK
     tiles = planes * per
-    columns = lax.dynamic_slice_in_dim(vertical, z * HEADS, HEADS, 0)
-    offsets = lax.dynamic_slice_in_dim(slash, z * HEADS, HEADS, 0)
-    tile = jnp.arange(tiles, dtype=jnp.int32)
+    slots = SLOTS // 2
+    tile = lax.broadcasted_iota(jnp.int32, (tiles, slots), 0)
     strip = ((y * planes + tile // per) * across + x) * cores + core
     blocks = strip * per + tile % per
-    sources = blocks[None, :, None] - offsets[:, None, :]
-    repeated = jnp.any(sources[..., None] == columns[:, None, None, :], axis=-1)
-    keep_source = (offsets >= 0)[:, None, :] & (sources >= 0)
-    keep_source &= (offsets == 0)[:, None, :] | ~repeated
-    spread = jnp.broadcast_to(columns[:, None, :], sources.shape)
-    keep_column = (spread >= 0) & (spread < blocks[None, :, None])
-    picks = jnp.concatenate([sources, spread], axis=-1).reshape(HEADS * tiles, SLOTS)
-    keep = jnp.concatenate([keep_source, keep_column], axis=-1).reshape(HEADS * tiles, SLOTS)
-    slot = jnp.arange(SLOTS, dtype=jnp.int32)
-    place = jnp.sum((keep[:, None, :] & (slot[None, :] < slot[:, None])[None]).astype(jnp.int32), -1)
-    half = picks % per
-    strip = picks // per
-    core_of = (strip + core) % cores
-    x_of = ring_slot(strip // cores - x, across)
-    z_of = strip // (cores * across) % planes
-    y_of = ring_slot(strip // (cores * across * planes) - y, reps)
-    where = ((((core_of * reps + y_of) * across + x_of) * planes + z_of) * per + half) * BLOCK
-    hit = keep[:, None, :] & (place[:, None, :] == slot[None, :, None])
-    idx = jnp.sum(jnp.where(hit, where[:, None, :], 0), axis=-1)
-    return idx, jnp.sum(keep.astype(jnp.int32), axis=-1)
+    earlier = lax.broadcasted_iota(jnp.int32, (slots, slots), 0) < lax.broadcasted_iota(
+        jnp.int32, (slots, slots), 1
+    )
+    earlier = earlier.astype(jnp.float32)
+    slot = lax.broadcasted_iota(jnp.int32, (tiles, SLOTS), 1)
+    first = pl.multiple_of(z * HEADS, HEADS)
+    vertical = vertical_ref[pl.ds(first, HEADS), :]
+    slash = slash_ref[pl.ds(first, HEADS), :]
+
+    def place_of(picks):
+        picks = jnp.maximum(picks, 0)
+        strip = picks // per
+        core_of = (strip + core) % cores
+        x_of = ring_slot(strip // cores - x + across, across)
+        z_of = strip // (cores * across) % planes
+        y_of = ring_slot(strip // (cores * across * planes) - y + reps, reps)
+        at = ((core_of * reps + y_of) * across + x_of) * planes + z_of
+        return (at * per + picks % per) * BLOCK
+
+    for head in range(HEADS):
+        columns = jnp.broadcast_to(vertical[head : head + 1], (tiles, slots))
+        offsets = jnp.broadcast_to(slash[head : head + 1], (tiles, slots))
+        sources = blocks - offsets
+        repeated = jnp.zeros((tiles, slots), jnp.int32)
+        for j in range(slots):
+            same = sources == vertical_s[z * HEADS + head, j]
+            repeated = jnp.where(same, 1, repeated)
+        keep = (offsets >= 0) & (sources >= 0) & ((offsets == 0) | (repeated == 0))
+        total = jnp.zeros((tiles, 1), jnp.int32)
+        idx = jnp.zeros((tiles, SLOTS), jnp.int32)
+        for picks, ok in ((sources, keep), (columns, (columns >= 0) & (columns < blocks))):
+            taken = jnp.where(ok, 1.0, 0.0)
+            before = jnp.dot(taken, earlier, preferred_element_type=jnp.float32)
+            goes = jnp.where(ok, before.astype(jnp.int32) + total, -1)
+            at = place_of(picks)
+            for j in range(slots):
+                hit = goes[:, j : j + 1] == slot
+                idx = jnp.where(hit, at[:, j : j + 1], idx)
+            total = total + jnp.sum(taken, axis=1, keepdims=True).astype(jnp.int32)
+        rows = pl.ds(head * tiles, tiles)
+        idx_ref[rows, :] = idx
+        count_ref[rows, :] = jnp.broadcast_to(total, (tiles, 8))
+
+
+def block_lists(vertical, slash, sizes):
+    tiles = sizes[0] * ROWS // BLOCK
+    vmem = pl.BlockSpec(memory_space=pltpu.VMEM)
+    return pl.pallas_call(
+        functools.partial(list_kernel, sizes),
+        out_shape=(
+            jax.ShapeDtypeStruct((HEADS * tiles, SLOTS), jnp.int32),
+            jax.ShapeDtypeStruct((HEADS * tiles, 8), jnp.int32),
+        ),
+        in_specs=[pl.BlockSpec(memory_space=pltpu.SMEM), vmem, vmem],
+        out_specs=(vmem, vmem),
+    )(vertical, vertical, slash)
 
 
 def body(sizes, queries, keys, values, vertical, slash):

time: 237 us -> 225 us (0.949); the launches traced: 237 us -> 221 us
  Pallas kernels: 65.3 us -> 55.5 us
  blocking collectives: 58.1 us -> 64.9 us
  waiting for transfers between devices: 40.3 us -> 34.8 us
  local copies, waits for them, and re-layouts: 30.9 us -> 26.4 us
  other arithmetic: 5.44 us -> 1.49 us
    pallas_call x2, Pallas kernels: 65.3 us -> 50.4 us  [attend(): pl.pallas_call(functools.partial(attend_kernel, tiles, first_head, heads,...]
    all_to_all x2, blocking collectives: 58.1 us -> 64.9 us  [regroup(): return lax.all_to_all(x, 'z', split_axis=0, concat_axis=0, tiled=True)]
    ppermute x26, waiting for transfers between devices: 40.2 us -> 34.7 us  [shifted(): return lax.ppermute(x, axis, [(i, (i + by) % size) for i in range(size)])]
    pallas_call x0 -> x1, Pallas kernels: none -> 5.11 us  [block_lists(): pl.pallas_call(functools.partial(list_kernel, sizes), out_shape=(jax.Shap...]
    reduce_or x1 -> x0, other arithmetic: 2.79 us -> none  [block_lists(): repeated = jnp.any(sources[..., None] == columns[:, None, None, :], axis=-1)]
    unnamed x50 -> x52, local copies, waits for them, and re-layouts: 17.5 us -> 16.5 us
  transfers between devices with their start and end apart: 28 -> 28, of which waited for: 13 -> 13; matrix products, arithmetic and copies ran while one was open for 7% -> 5% of each run, Pallas kernels for 15% -> 14%
where the time goes in v2:
time: 225 us; the launch traced here: 221 us
  blocking collectives  64.9 us (29%)
  Pallas kernels  55.5 us (25%)
  starting transfers between devices  37.7 us (17%)
  waiting for transfers between devices  34.8 us (15%)
  local copies, waits for them, and re-layouts  26.4 us (12%)
    all_to_all x2, blocking collectives, regroup(): return lax.all_to_all(x, 'z', split_axis=0, concat_axis=0, tiled=True)  64.9 us
    pallas_call x2, Pallas kernels, attend(): pl.pallas_call(functools.partial(attend_kernel, tiles, first_head, heads,...  50.4 us
    ppermute x26, waiting for transfers between devices, shifted(): return lax.ppermute(x, axis, [(i, (i + by) % size) for i in range(size)])  34.7 us
    ppermute x26, starting transfers between devices, shifted(): return lax.ppermute(x, axis, [(i, (i + by) % size) for i in range(size)])  19.3 us
    all_to_all x2, starting transfers between devices, regroup(): return lax.all_to_all(x, 'z', split_axis=0, concat_axis=0, tiled=True)  18.4 us
    unnamed x52, local copies, waits for them, and re-layouts  16.5 us
    pallas_call x1, Pallas kernels, block_lists(): pl.pallas_call(functools.partial(list_kernel, sizes), out_shape=(jax.Shap...  5.11 us
  transfers between devices with their start and end apart: 28, of which 13 were waited for; matrix products, arithmetic and copies ran while one was open for 5% of the time, Pallas kernels for 14%

profile of v2, /device:TPU:30, one launch (start us, length us, event | category | flops | bytes accessed | tf_op | source)
XLA Modules:
  0.0 221.1 jit_solution(15560068407136429006)
XLA Ops:
  2.1 25.8 %all_to_all.20 = bf16[8,256,128]{2,1,0:T(8,128)(2,1)S(1)} all-to-all(bf16[8,256,128]{2,1,0:T(8,128)(2,1)S(1)} %pad_maximum_fusion), channel_id=1, replica_groups=mesh['z'=8,'x'=4,'core'=2,'rep'=4] {'z'}, dimensions={0} | all-to-all | bytes 1048576 | tf_op jit(solution)/shard_map/all_to_all | solution.py:279
  28.4 1.5 collective-permute-start.1
  30.2 1.8 collective-permute-start.3
  32.0 2.3 %collective-permute-done = bf16[1024,128]{1,0:T(8,128)(2,1)S(1)} collective-permute-done((bf16[1024,128]{1,0:T(8,128)(2,1)S(1)}, bf16[1024,128]{1,0:T(8,128)(2,1)S(1)}, u32[]{:S(2)}, u32[]{:S(2)}) %collective-permute-start) | collective-permute-done | bytes 262176 | tf_op jit(solution)/shard_map/ppermute | solution.py:182
  34.3 1.7 collective-permute-done.1
  36.4 1.4 collective-permute-done.3
  37.9 1.8 collective-permute-start.4
  40.5 1.7 collective-permute-start.7
  44.4 1.5 collective-permute-done.5
  48.5 1.5 copy.20
  50.0 4.5 %all-to-all-start.1 = ((bf16[8,128,1024]{2,1,0:T(8,128)(2,1)}), bf16[8,128,1024]{2,1,0:T(8,128)(2,1)}, u32[]{:S(2)}, u32[]{:S(2)}) async-start(bf16[8,128,1024]{2,1,0:T(8,128)(2,1)} %bitcast.32), calls=%async_computation.1 | async-start | bytes 4194304 | tf_op jit(solution)/shard_map/all_to_all | solution.py:279
  54.5 1.7 collective-permute-start.9
  56.2 2.9 %collective-permute-start.10 = (bf16[4096,128]{1,0:T(8,128)(2,1)}, bf16[4096,128]{1,0:T(8,128)(2,1)}, u32[]{:S(2)}, u32[]{:S(2)}) collective-permute-start(bf16[4096,128]{1,0:T(8,128)(2,1)} %constant_dynamic-update-slice_fusion.5.refs_10_), channel_id=1, source_target_pairs={{0,8},{8,16},{16,24},{24,0},{1,9},{9,17},{17,25},{25,1},{2,10},{10... | collective-permute-start | bytes 3145736 | tf_op jit(solution)/shard_map/ppermute | solution.py:182
  59.1 8.4 %collective-permute-done.8.refs_1_ = bf16[4096,128]{1,0:T(8,128)(2,1)S(1)} collective-permute-done((bf16[4096,128]{1,0:T(8,128)(2,1)S(1)}, bf16[4096,128]{1,0:T(8,128)(2,1)S(1)}, u32[]{:S(2)}, u32[]{:S(2)}) %collective-permute-start.8) | collective-permute-done | bytes 1048608 | tf_op jit(solution)/shard_map/ppermute | solution.py:182
  69.0 5.1 %shard_map.55 = (s32[128,48]{1,0:T(8,128)}, s32[128,8]{1,0:T(8,128)}) custom-call(s32[64,24]{1,0:T(8,128)} %copy.8.vertical_s.vertical_ref, s32[64,24]{1,0:T(8,128)} %copy.8.vertical_s.vertical_ref, s32[64,24]{1,0:T(8,128)} %copy.10.slash_ref), custom_call_target="tpu_custom_call" | custom-call | tf_op jit(solution)/shard_map/pallas_call | solution.py:263
  75.8 3.4 %collective-permute-done.11.refs_12_ = bf16[4096,128]{1,0:T(8,128)(2,1)} collective-permute-done((bf16[4096,128]{1,0:T(8,128)(2,1)}, bf16[4096,128]{1,0:T(8,128)(2,1)}, u32[]{:S(2)}, u32[]{:S(2)}) %collective-permute-start.11) | collective-permute-done | bytes 1048608 | tf_op jit(solution)/shard_map/ppermute | solution.py:182
  79.3 1.9 collective-permute-start.14
  81.5 1.1 slice.45
  84.1 1.8 collective-permute-start.19
  85.9 2.7 %collective-permute-done.14.refs_3_ = bf16[2048,128]{1,0:T(8,128)(2,1)S(1)} collective-permute-done((bf16[2048,128]{1,0:T(8,128)(2,1)S(1)}, bf16[2048,128]{1,0:T(8,128)(2,1)S(1)}, u32[]{:S(2)}, u32[]{:S(2)}) %collective-permute-start.14) | collective-permute-done | bytes 524320 | tf_op jit(solution)/shard_map/ppermute | solution.py:182
  88.6 8.4 %collective-permute-done.15.refs_4_ = bf16[2048,128]{1,0:T(8,128)(2,1)} collective-permute-done((bf16[2048,128]{1,0:T(8,128)(2,1)S(1)}, bf16[2048,128]{1,0:T(8,128)(2,1)}, u32[]{:S(2)}, u32[]{:S(2)}) %collective-permute-start.15) | collective-permute-done | bytes 524320 | tf_op jit(solution)/shard_map/ppermute | solution.py:182
  97.5 1.8 collective-permute-done.19.refs_14_
  104.0 2.8 %fusion = (bf16[1024,512]{1,0:T(8,128)(2,1)}, bf16[1024,512]{1,0:T(8,128)(2,1)S(1)}) fusion(bf16[1024,1024]{1,0:T(8,128)(2,1)} %bitcast.5), kind=kLoop, calls=%fused_computation.15 | loop fusion | bytes 4194304 | tf_op jit(solution)/shard_map/slice | solution.py:299
  106.9 23.8 %shard_map.57 = bf16[1024,512]{1,0:T(8,128)(2,1)S(1)} custom-call(s32[128,48]{1,0:T(8,128)S(1)} %copy-done.16, s32[128,8]{1,0:T(8,128)S(1)} %copy-done.17, bf16[1024,512]{1,0:T(8,128)(2,1)S(1)} %get-tuple-element.64.query_ref, bf16[4096,128]{1,0:T(8,128)(2,1)S(1)} %constant_dynamic-update-slice_fusion.refs_0_, ...), custom_call_target="tpu_custom_call" | custom-call | tf_op jit(solution)/shard_map/pallas_call | solution.py:163
  131.7 13.9 %all-to-all-start.3 = ((bf16[8,128,512]{2,1,0:T(8,128)(2,1)}), bf16[8,128,512]{2,1,0:T(8,128)(2,1)}, u32[]{:S(2)}, u32[]{:S(2)}) async-start(bf16[8,128,512]{2,1,0:T(8,128)(2,1)} %bitcast.30), calls=%async_computation.3 | async-start | bytes 2097152 | tf_op jit(solution)/shard_map/all_to_all | solution.py:279
  145.6 1.2 copy-done.3
  146.8 1.2 copy-done.6
  148.1 1.2 copy-done.9
  151.4 26.6 %shard_map.56 = bf16[1024,512]{1,0:T(8,128)(2,1)S(1)} custom-call(s32[128,48]{1,0:T(8,128)S(1)} %copy-done.16, s32[128,8]{1,0:T(8,128)S(1)} %copy-done.17, bf16[1024,512]{1,0:T(8,128)(2,1)S(1)} %copy-done.9, bf16[4096,128]{1,0:T(8,128)(2,1)S(1)} %constant_dynamic-update-slice_fusion.refs_0_, bf16[4096,128]{1,0:T(8,128)(2,1)S(1)} %collective-permute-done.8.refs_1_, ...), custom_call_target="tpu_custom_call" | custom-call | tf_op jit(solution)/shard_map/pallas_call | solution.py:163
  178.9 39.1 %all_to_all.21 = bf16[8,128,512]{2,1,0:T(8,128)(2,1)S(1)} all-to-all(bf16[8,128,512]{2,1,0:T(8,128)(2,1)} %bitcast.31), channel_id=1, replica_groups=mesh['z'=8,'x'=4,'core'=2,'rep'=4] {'z'}, dimensions={0} | all-to-all | bytes 2097152 | tf_op jit(solution)/shard_map/all_to_all | solution.py:279
  218.0 1.5 maximum_bitcast_fusion
  219.5 1.6 copy.16
  (98 shorter events, 22.9 us)
Async XLA Ops:
  27.9 6.4 %collective-permute-start = (bf16[1024,128]{1,0:T(8,128)(2,1)S(1)}, bf16[1024,128]{1,0:T(8,128)(2,1)S(1)}, u32[]{:S(2)}, u32[]{:S(2)}) collective-permute-start(bf16[1024,128]{1,0:T(8,128)(2,1)S(1)} %bitcast.37), channel_id=1, source_target_pairs={{0,8},{8,16},{16,24},{24,0},{1,9},{9,17},{17,25},{25,1},{2,10},{10... | collective-permute-start | bytes 786440 | tf_op jit(solution)/shard_map/ppermute | solution.py:182
  28.4 7.6 %collective-permute-start.1 = (bf16[1024,128]{1,0:T(8,128)(2,1)S(1)}, bf16[1024,128]{1,0:T(8,128)(2,1)S(1)}, u32[]{:S(2)}, u32[]{:S(2)}) collective-permute-start(bf16[1024,128]{1,0:T(8,128)(2,1)S(1)} %bitcast.38), channel_id=1, source_target_pairs={{0,24},{8,0},{16,8},{24,16},{1,25},{9,1},{17,9},{25,17},{2,26},{10... | collective-permute-start | bytes 786440 | tf_op jit(solution)/shard_map/ppermute | solution.py:182
  30.0 6.4 %collective-permute-start.2 = (bf16[1024,128]{1,0:T(8,128)(2,1)S(1)}, bf16[1024,128]{1,0:T(8,128)(2,1)S(1)}, u32[]{:S(2)}, u32[]{:S(2)}) collective-permute-start(bf16[1024,128]{1,0:T(8,128)(2,1)S(1)} %bitcast.34), channel_id=1, source_target_pairs={{0,1},{1,2},{2,3},{3,0},{4,5},{5,6},{6,7},{7,4},{8,9},{9,10},{10,1... | collective-permute-start | bytes 786440 | tf_op jit(solution)/shard_map/ppermute | solution.py:182
  30.2 7.6 %collective-permute-start.3 = (bf16[1024,128]{1,0:T(8,128)(2,1)S(1)}, bf16[1024,128]{1,0:T(8,128)(2,1)S(1)}, u32[]{:S(2)}, u32[]{:S(2)}) collective-permute-start(bf16[1024,128]{1,0:T(8,128)(2,1)S(1)} %bitcast.35), channel_id=1, source_target_pairs={{0,3},{1,0},{2,1},{3,2},{4,7},{5,4},{6,5},{7,6},{8,11},{9,8},{10,9... | collective-permute-start | bytes 786440 | tf_op jit(solution)/shard_map/ppermute | solution.py:182
  37.9 10.6 %copy-start.18 = (bf16[128,8192]{1,0:T(8,128)(2,1)S(1)}, bf16[128,8192]{1,0:T(8,128)(2,1)}, u32[]{:S(2)}) copy-start(bf16[128,8192]{1,0:T(8,128)(2,1)} %param.5) | copy-start | bytes 6291460
  37.9 6.5 %collective-permute-start.4 = (bf16[512,128]{1,0:T(8,128)(2,1)S(1)}, bf16[512,128]{1,0:T(8,128)(2,1)S(1)}, u32[]{:S(2)}, u32[]{:S(2)}) collective-permute-start(bf16[512,128]{1,0:T(8,128)(2,1)S(1)} %slice.38), channel_id=1, source_target_pairs={{0,8},{8,16},{16,24},{24,0},{1,9},{9,17},{17,25},{25,1},{2,10},{10... | collective-permute-start | bytes 393224 | tf_op jit(solution)/shard_map/ppermute | solution.py:182
  39.7 6.2 %collective-permute-start.5 = (bf16[512,128]{1,0:T(8,128)(2,1)S(1)}, bf16[512,128]{1,0:T(8,128)(2,1)S(1)}, u32[]{:S(2)}, u32[]{:S(2)}) collective-permute-start(bf16[512,128]{1,0:T(8,128)(2,1)S(1)} %slice.39), channel_id=1, source_target_pairs={{0,24},{8,0},{16,8},{24,16},{1,25},{9,1},{17,9},{25,17},{2,26},{10... | collective-permute-start | bytes 393224 | tf_op jit(solution)/shard_map/ppermute | solution.py:182
  40.1 5.8 %collective-permute-start.6 = (bf16[512,128]{1,0:T(8,128)(2,1)S(1)}, bf16[512,128]{1,0:T(8,128)(2,1)S(1)}, u32[]{:S(2)}, u32[]{:S(2)}) collective-permute-start(bf16[512,128]{1,0:T(8,128)(2,1)S(1)} %slice.40), channel_id=1, source_target_pairs={{0,1},{1,2},{2,3},{3,0},{4,5},{5,6},{6,7},{7,4},{8,9},{9,10},{10,1... | collective-permute-start | bytes 393224 | tf_op jit(solution)/shard_map/ppermute | solution.py:182
  40.5 6.3 %collective-permute-start.7 = (bf16[512,128]{1,0:T(8,128)(2,1)S(1)}, bf16[512,128]{1,0:T(8,128)(2,1)S(1)}, u32[]{:S(2)}, u32[]{:S(2)}) collective-permute-start(bf16[512,128]{1,0:T(8,128)(2,1)S(1)} %slice.41), channel_id=1, source_target_pairs={{0,3},{1,0},{2,1},{3,2},{4,7},{5,4},{6,5},{7,6},{8,11},{9,8},{10,9... | collective-permute-start | bytes 393224 | tf_op jit(solution)/shard_map/ppermute | solution.py:182
  48.1 19.4 %collective-permute-start.8 = (bf16[4096,128]{1,0:T(8,128)(2,1)S(1)}, bf16[4096,128]{1,0:T(8,128)(2,1)S(1)}, u32[]{:S(2)}, u32[]{:S(2)}) collective-permute-start(bf16[4096,128]{1,0:T(8,128)(2,1)S(1)} %constant_dynamic-update-slice_fusion.refs_0_), channel_id=1, source_target_pairs={{0,1},{1,2},{2,3},{3,0},{4,5},{5,6},{6,7},{7,4},{8,9},{9,10},{10,1... | collective-permute-start | bytes 3145736 | tf_op jit(solution)/shard_map/ppermute | solution.py:182
  50.0 17.6 %copy-start.19 = (s32[64,24]{0,1:T(8,128)S(1)}, s32[64,24]{0,1:T(8,128)}, u32[]{:S(2)}) copy-start(s32[64,24]{0,1:T(8,128)} %param.8) | copy-start | bytes 18436
  50.0 18.3 %copy-start.20 = (s32[64,24]{0,1:T(8,128)S(1)}, s32[64,24]{0,1:T(8,128)}, u32[]{:S(2)}) copy-start(s32[64,24]{0,1:T(8,128)} %param.9) | copy-start | bytes 18436
  50.0 53.9 %all-to-all-start.1 = ((bf16[8,128,1024]{2,1,0:T(8,128)(2,1)}), bf16[8,128,1024]{2,1,0:T(8,128)(2,1)}, u32[]{:S(2)}, u32[]{:S(2)}) async-start(bf16[8,128,1024]{2,1,0:T(8,128)(2,1)} %bitcast.32), calls=%async_computation.1 | async-start | bytes 4194304 | tf_op jit(solution)/shard_map/all_to_all | solution.py:279
  54.5 20.4 %collective-permute-start.9 = (bf16[4096,128]{1,0:T(8,128)(2,1)S(1)}, bf16[4096,128]{1,0:T(8,128)(2,1)S(1)}, u32[]{:S(2)}, u32[]{:S(2)}) collective-permute-start(bf16[4096,128]{1,0:T(8,128)(2,1)S(1)} %constant_dynamic-update-slice_fusion.refs_0_), channel_id=1, source_target_pairs={{0,3},{1,0},{2,1},{3,2},{4,7},{5,4},{6,5},{7,6},{8,11},{9,8},{10,9... | collective-permute-start | bytes 3145736 | tf_op jit(solution)/shard_map/ppermute | solution.py:182
  56.2 19.6 %collective-permute-start.10 = (bf16[4096,128]{1,0:T(8,128)(2,1)}, bf16[4096,128]{1,0:T(8,128)(2,1)}, u32[]{:S(2)}, u32[]{:S(2)}) collective-permute-start(bf16[4096,128]{1,0:T(8,128)(2,1)} %constant_dynamic-update-slice_fusion.5.refs_10_), channel_id=1, source_target_pairs={{0,8},{8,16},{16,24},{24,0},{1,9},{9,17},{17,25},{25,1},{2,10},{10... | collective-permute-start | bytes 3145736 | tf_op jit(solution)/shard_map/ppermute | solution.py:182
  59.1 20.1 %collective-permute-start.11 = (bf16[4096,128]{1,0:T(8,128)(2,1)}, bf16[4096,128]{1,0:T(8,128)(2,1)}, u32[]{:S(2)}, u32[]{:S(2)}) collective-permute-start(bf16[4096,128]{1,0:T(8,128)(2,1)} %constant_dynamic-update-slice_fusion.5.refs_10_), channel_id=1, source_target_pairs={{0,24},{8,0},{16,8},{24,16},{1,25},{9,1},{17,9},{25,17},{2,26},{10... | collective-permute-start | bytes 3145736 | tf_op jit(solution)/shard_map/ppermute | solution.py:182
  59.1 20.1 %collective-permute-start.12 = (bf16[4096,128]{1,0:T(8,128)(2,1)S(1)}, bf16[4096,128]{1,0:T(8,128)(2,1)}, u32[]{:S(2)}, u32[]{:S(2)}) collective-permute-start(bf16[4096,128]{1,0:T(8,128)(2,1)S(1)} %constant_dynamic-update-slice_fusion.refs_0_), channel_id=1, source_target_pairs={{0,4},{4,0},{1,5},{5,1},{2,6},{6,2},{3,7},{7,3},{8,12},{12,8},{9,1... | collective-permute-start | bytes 3145736 | tf_op jit(solution)/shard_map/ppermute | solution.py:182
  67.6 11.7 %collective-permute-start.13 = (bf16[4096,128]{1,0:T(8,128)(2,1)}, bf16[4096,128]{1,0:T(8,128)(2,1)}, u32[]{:S(2)}, u32[]{:S(2)}) collective-permute-start(bf16[4096,128]{1,0:T(8,128)(2,1)} %constant_dynamic-update-slice_fusion.5.refs_10_), channel_id=1, source_target_pairs={{0,4},{4,0},{1,5},{5,1},{2,6},{6,2},{3,7},{7,3},{8,12},{12,8},{9,1... | collective-permute-start | bytes 3145736 | tf_op jit(solution)/shard_map/ppermute | solution.py:182
  79.3 9.3 %collective-permute-start.14 = (bf16[2048,128]{1,0:T(8,128)(2,1)S(1)}, bf16[2048,128]{1,0:T(8,128)(2,1)S(1)}, u32[]{:S(2)}, u32[]{:S(2)}) collective-permute-start(bf16[2048,128]{1,0:T(8,128)(2,1)S(1)} %slice.43), channel_id=1, source_target_pairs={{0,1},{1,2},{2,3},{3,0},{4,5},{5,6},{6,7},{7,4},{8,9},{9,10},{10,1... | collective-permute-start | bytes 1572872 | tf_op jit(solution)/shard_map/ppermute | solution.py:182
  81.2 18.9 %collective-permute-start.16 = (bf16[4096,128]{1,0:T(8,128)(2,1)S(1)}, bf16[4096,128]{1,0:T(8,128)(2,1)S(1)}, u32[]{:S(2)}, u32[]{:S(2)}) collective-permute-start(bf16[4096,128]{1,0:T(8,128)(2,1)S(1)} %collective-permute-done.8.refs_1_), channel_id=1, source_target_pairs={{0,4},{4,0},{1,5},{5,1},{2,6},{6,2},{3,7},{7,3},{8,12},{12,8},{9,1... | collective-permute-start | bytes 3145736 | tf_op jit(solution)/shard_map/ppermute | solution.py:182
  81.3 15.7 %collective-permute-start.15 = (bf16[2048,128]{1,0:T(8,128)(2,1)S(1)}, bf16[2048,128]{1,0:T(8,128)(2,1)}, u32[]{:S(2)}, u32[]{:S(2)}) collective-permute-start(bf16[2048,128]{1,0:T(8,128)(2,1)S(1)} %slice.44), channel_id=1, source_target_pairs={{0,3},{1,0},{2,1},{3,2},{4,7},{5,4},{6,5},{7,6},{8,11},{9,8},{10,9... | collective-permute-start | bytes 1572872 | tf_op jit(solution)/shard_map/ppermute | solution.py:182
  82.6 14.4 %collective-permute-start.18 = (bf16[2048,128]{1,0:T(8,128)(2,1)S(1)}, bf16[2048,128]{1,0:T(8,128)(2,1)}, u32[]{:S(2)}, u32[]{:S(2)}) collective-permute-start(bf16[2048,128]{1,0:T(8,128)(2,1)S(1)} %slice.45), channel_id=1, source_target_pairs={{0,8},{8,16},{16,24},{24,0},{1,9},{9,17},{17,25},{25,1},{2,10},{10... | collective-permute-start | bytes 1572872 | tf_op jit(solution)/shard_map/ppermute | solution.py:182
  84.1 15.3 %collective-permute-start.19 = (bf16[2048,128]{1,0:T(8,128)(2,1)S(1)}, bf16[2048,128]{1,0:T(8,128)(2,1)}, u32[]{:S(2)}, u32[]{:S(2)}) collective-permute-start(bf16[2048,128]{1,0:T(8,128)(2,1)S(1)} %slice.46), channel_id=1, source_target_pairs={{0,24},{8,0},{16,8},{24,16},{1,25},{9,1},{17,9},{25,17},{2,26},{10... | collective-permute-start | bytes 1572872 | tf_op jit(solution)/shard_map/ppermute | solution.py:182
  88.6 13.1 %collective-permute-start.17 = (bf16[4096,128]{1,0:T(8,128)(2,1)S(1)}, bf16[4096,128]{1,0:T(8,128)(2,1)S(1)}, u32[]{:S(2)}, u32[]{:S(2)}) collective-permute-start(bf16[4096,128]{1,0:T(8,128)(2,1)S(1)} %collective-permute-done.9.refs_2_), channel_id=1, source_target_pairs={{0,4},{4,0},{1,5},{5,1},{2,6},{6,2},{3,7},{7,3},{8,12},{12,8},{9,1... | collective-permute-start | bytes 3145736 | tf_op jit(solution)/shard_map/ppermute | solution.py:182
  97.0 9.8 %collective-permute-start.22 = (bf16[4096,128]{1,0:T(8,128)(2,1)}, bf16[4096,128]{1,0:T(8,128)(2,1)}, u32[]{:S(2)}, u32[]{:S(2)}) collective-permute-start(bf16[4096,128]{1,0:T(8,128)(2,1)} %collective-permute-done.10.refs_11_), channel_id=1, source_target_pairs={{0,4},{4,0},{1,5},{5,1},{2,6},{6,2},{3,7},{7,3},{8,12},{12,8},{9,1... | collective-permute-start | bytes 3145736 | tf_op jit(solution)/shard_map/ppermute | solution.py:182
  97.0 9.8 %collective-permute-start.23 = (bf16[4096,128]{1,0:T(8,128)(2,1)}, bf16[4096,128]{1,0:T(8,128)(2,1)}, u32[]{:S(2)}, u32[]{:S(2)}) collective-permute-start(bf16[4096,128]{1,0:T(8,128)(2,1)} %collective-permute-done.11.refs_12_), channel_id=1, source_target_pairs={{0,4},{4,0},{1,5},{5,1},{2,6},{6,2},{3,7},{7,3},{8,12},{12,8},{9,1... | collective-permute-start | bytes 3145736 | tf_op jit(solution)/shard_map/ppermute | solution.py:182
  99.4 3.3 %collective-permute-start.20 = (bf16[2048,128]{1,0:T(8,128)(2,1)S(1)}, bf16[2048,128]{1,0:T(8,128)(2,1)S(1)}, u32[]{:S(2)}, u32[]{:S(2)}) collective-permute-start(bf16[2048,128]{1,0:T(8,128)(2,1)S(1)} %collective-permute-done.14.refs_3_), channel_id=1, source_target_pairs={{0,4},{4,0},{1,5},{5,1},{2,6},{6,2},{3,7},{7,3},{8,12},{12,8},{9,1... | collective-permute-start | bytes 1572872 | tf_op jit(solution)/shard_map/ppermute | solution.py:182
  101.2 5.6 %collective-permute-start.21 = (bf16[2048,128]{1,0:T(8,128)(2,1)}, bf16[2048,128]{1,0:T(8,128)(2,1)}, u32[]{:S(2)}, u32[]{:S(2)}) collective-permute-start(bf16[2048,128]{1,0:T(8,128)(2,1)} %collective-permute-done.15.refs_4_), channel_id=1, source_target_pairs={{0,4},{4,0},{1,5},{5,1},{2,6},{6,2},{3,7},{7,3},{8,12},{12,8},{9,1... | collective-permute-start | bytes 1572872 | tf_op jit(solution)/shard_map/ppermute | solution.py:182
  102.6 4.2 %collective-permute-start.24 = (bf16[2048,128]{1,0:T(8,128)(2,1)}, bf16[2048,128]{1,0:T(8,128)(2,1)}, u32[]{:S(2)}, u32[]{:S(2)}) collective-permute-start(bf16[2048,128]{1,0:T(8,128)(2,1)} %collective-permute-done.18.refs_13_), channel_id=1, source_target_pairs={{0,4},{4,0},{1,5},{5,1},{2,6},{6,2},{3,7},{7,3},{8,12},{12,8},{9,1... | collective-permute-start | bytes 1572872 | tf_op jit(solution)/shard_map/ppermute | solution.py:182
  103.4 3.4 %collective-permute-start.25 = (bf16[2048,128]{1,0:T(8,128)(2,1)}, bf16[2048,128]{1,0:T(8,128)(2,1)}, u32[]{:S(2)}, u32[]{:S(2)}) collective-permute-start(bf16[2048,128]{1,0:T(8,128)(2,1)} %collective-permute-done.19.refs_14_), channel_id=1, source_target_pairs={{0,4},{4,0},{1,5},{5,1},{2,6},{6,2},{3,7},{7,3},{8,12},{12,8},{9,1... | collective-permute-start | bytes 1572872 | tf_op jit(solution)/shard_map/ppermute | solution.py:182
  103.9 2.9 %copy-start.14 = (bf16[2048,128]{1,0:T(8,128)(2,1)S(1)}, bf16[2048,128]{1,0:T(8,128)(2,1)}, u32[]{:S(2)}) copy-start(bf16[2048,128]{1,0:T(8,128)(2,1)} %copy-done.13) | copy-start | bytes 1572868
  131.7 47.2 %all-to-all-start.3 = ((bf16[8,128,512]{2,1,0:T(8,128)(2,1)}), bf16[8,128,512]{2,1,0:T(8,128)(2,1)}, u32[]{:S(2)}, u32[]{:S(2)}) async-start(bf16[8,128,512]{2,1,0:T(8,128)(2,1)} %bitcast.30), calls=%async_computation.3 | async-start | bytes 2097152 | tf_op jit(solution)/shard_map/all_to_all | solution.py:279
  (17 other events, 26.6 us)

commit v3 on v2

--- a/solution.py
+++ b/solution.py
@@ -17,7 +17,7 @@
 SLOTS = 48
 TILES = 8
 CHUNK = 8
-HEAD_CUTS = (0, 4, 8)
+HEAD_CUTS = (0, 5, 8)
 NEG_FILL = -1e30
 SCALE = math.log2(math.e) / math.sqrt(HEAD_SIZE)
 

time: 225 us -> 234 us (1.040); the launches traced: 221 us -> 237 us
  Pallas kernels: 55.5 us -> 72.4 us
  starting transfers between devices: 37.7 us -> 34.7 us
    pallas_call x2, Pallas kernels: 50.4 us -> 67.3 us  [attend(): pl.pallas_call(functools.partial(attend_kernel, tiles, first_head, heads,...]
    all_to_all x2, starting transfers between devices: 18.4 us -> 15.7 us  [regroup(): return lax.all_to_all(x, 'z', split_axis=0, concat_axis=0, tiled=True)]
    unnamed x52 -> x48, local copies, waits for them, and re-layouts: 16.5 us -> 16.8 us
  transfers between devices with their start and end apart: 28 -> 28, of which waited for: 13 -> 15; matrix products, arithmetic and copies ran while one was open for 5% -> 4% of each run, Pallas kernels for 14% -> 20%
where the time goes in v3:
time: 234 us; the launch traced here: 237 us
  Pallas kernels  72.4 us (31%)
  blocking collectives  65.5 us (28%)
  waiting for transfers between devices  35.8 us (15%)
  starting transfers between devices  34.7 us (15%)
  local copies, waits for them, and re-layouts  27.4 us (12%)
    pallas_call x2, Pallas kernels, attend(): pl.pallas_call(functools.partial(attend_kernel, tiles, first_head, heads,...  67.3 us
    all_to_all x2, blocking collectives, regroup(): return lax.all_to_all(x, 'z', split_axis=0, concat_axis=0, tiled=True)  65.5 us
    ppermute x26, waiting for transfers between devices, shifted(): return lax.ppermute(x, axis, [(i, (i + by) % size) for i in range(size)])  35.8 us
    ppermute x26, starting transfers between devices, shifted(): return lax.ppermute(x, axis, [(i, (i + by) % size) for i in range(size)])  19 us
    unnamed x48, local copies, waits for them, and re-layouts  16.8 us
    all_to_all x2, starting transfers between devices, regroup(): return lax.all_to_all(x, 'z', split_axis=0, concat_axis=0, tiled=True)  15.7 us
    pallas_call x1, Pallas kernels, block_lists(): pl.pallas_call(functools.partial(list_kernel, sizes), out_shape=(jax.Shap...  5.08 us
  transfers between devices with their start and end apart: 28, of which 15 were waited for; matrix products, arithmetic and copies ran while one was open for 4% of the time, Pallas kernels for 20%

profile of v3, /device:TPU:30, one launch (start us, length us, event | category | flops | bytes accessed | tf_op | source)
XLA Modules:
  0.0 237.5 jit_solution(531998980304049760)
XLA Ops:
  1.0 1.1 bitcast_bitcast_fusion.1
  2.1 25.8 %all_to_all.20 = bf16[8,256,128]{2,1,0:T(8,128)(2,1)S(1)} all-to-all(bf16[8,256,128]{2,1,0:T(8,128)(2,1)S(1)} %pad_maximum_fusion), channel_id=1, replica_groups=mesh['z'=8,'x'=4,'core'=2,'rep'=4] {'z'}, dimensions={0} | all-to-all | bytes 1048576 | tf_op jit(solution)/shard_map/all_to_all | solution.py:279
  28.4 1.5 collective-permute-start.1
  30.2 1.8 collective-permute-start.3
  32.0 2.3 collective-permute-done
  34.3 1.7 collective-permute-done.1
  36.4 1.4 collective-permute-done.3
  40.0 1.7 collective-permute-start.4
  42.5 1.7 collective-permute-start.7
  46.4 1.5 collective-permute-done.5
  51.7 1.5 copy.20
  53.2 4.5 %all-to-all-start.1 = ((bf16[8,128,1024]{2,1,0:T(8,128)(2,1)}), bf16[8,128,1024]{2,1,0:T(8,128)(2,1)}, u32[]{:S(2)}, u32[]{:S(2)}) async-start(bf16[8,128,1024]{2,1,0:T(8,128)(2,1)} %bitcast.29), calls=%async_computation.1 | async-start | bytes 4194304 | tf_op jit(solution)/shard_map/all_to_all | solution.py:279
  57.7 1.7 collective-permute-start.9
  59.5 2.9 %collective-permute-start.10 = (bf16[4096,128]{1,0:T(8,128)(2,1)}, bf16[4096,128]{1,0:T(8,128)(2,1)S(1)}, u32[]{:S(2)}, u32[]{:S(2)}) collective-permute-start(bf16[4096,128]{1,0:T(8,128)(2,1)} %constant_dynamic-update-slice_fusion.5.refs_10_), channel_id=1, source_target_pairs={{0,8},{8,16},{16,24},{24,0},{1,9},{9,17},{17,25},{25,1},{2,10},{10... | collective-permute-start | bytes 3145736 | tf_op jit(solution)/shard_map/ppermute | solution.py:182
  62.4 8.7 %collective-permute-done.8.refs_1_ = bf16[4096,128]{1,0:T(8,128)(2,1)S(1)} collective-permute-done((bf16[4096,128]{1,0:T(8,128)(2,1)}, bf16[4096,128]{1,0:T(8,128)(2,1)S(1)}, u32[]{:S(2)}, u32[]{:S(2)}) %collective-permute-start.8) | collective-permute-done | bytes 1048608 | tf_op jit(solution)/shard_map/ppermute | solution.py:182
  72.4 5.1 %shard_map.55 = (s32[128,48]{1,0:T(8,128)}, s32[128,8]{1,0:T(8,128)}) custom-call(s32[64,24]{1,0:T(8,128)} %copy.8.vertical_s.vertical_ref, s32[64,24]{1,0:T(8,128)} %copy.8.vertical_s.vertical_ref, s32[64,24]{1,0:T(8,128)} %copy.10.slash_ref), custom_call_target="tpu_custom_call" | custom-call | tf_op jit(solution)/shard_map/pallas_call | solution.py:263
  79.1 3.4 %collective-permute-done.11.refs_12_ = bf16[4096,128]{1,0:T(8,128)(2,1)} collective-permute-done((bf16[4096,128]{1,0:T(8,128)(2,1)}, bf16[4096,128]{1,0:T(8,128)(2,1)}, u32[]{:S(2)}, u32[]{:S(2)}) %collective-permute-start.11) | collective-permute-done | bytes 1048608 | tf_op jit(solution)/shard_map/ppermute | solution.py:182
  82.5 1.9 collective-permute-start.14
  85.1 1.1 slice.46
  86.2 1.9 collective-permute-start.19
  88.1 3.9 %collective-permute-done.14.refs_3_ = bf16[2048,128]{1,0:T(8,128)(2,1)S(1)} collective-permute-done((bf16[2048,128]{1,0:T(8,128)(2,1)S(1)}, bf16[2048,128]{1,0:T(8,128)(2,1)S(1)}, u32[]{:S(2)}, u32[]{:S(2)}) %collective-permute-start.14) | collective-permute-done | bytes 524320 | tf_op jit(solution)/shard_map/ppermute | solution.py:182
  92.0 8.3 %collective-permute-done.15.refs_4_ = bf16[2048,128]{1,0:T(8,128)(2,1)} collective-permute-done((bf16[2048,128]{1,0:T(8,128)(2,1)S(1)}, bf16[2048,128]{1,0:T(8,128)(2,1)}, u32[]{:S(2)}, u32[]{:S(2)}) %collective-permute-start.15) | collective-permute-done | bytes 524320 | tf_op jit(solution)/shard_map/ppermute | solution.py:182
  106.2 1.3 slice.51.query_ref
  108.2 1.2 copy-done.5
  109.5 1.0 copy-done.9
  111.5 24.2 %shard_map.57 = bf16[1024,384]{1,0:T(8,128)(2,1)S(1)} custom-call(s32[128,48]{1,0:T(8,128)S(1)} %copy-done.14, s32[128,8]{1,0:T(8,128)S(1)} %copy-done.15, bf16[1024,384]{1,0:T(8,128)(2,1)S(1)} %slice.51.query_ref, bf16[4096,128]{1,0:T(8,128)(2,1)} %constant_dynamic-update-slice_fusion.refs_0_, bf16[4096,128]{1,0:T(8,128)(2,1)S(1)} %collective-permute-done.8.refs_1_, ...), custom_call_target="tpu_custom_call" | custom-call | tf_op jit(solution)/shard_map/pallas_call | solution.py:163
  136.7 11.3 %all-to-all-start.3 = ((bf16[8,128,384]{2,1,0:T(8,128)(2,1)}), bf16[8,128,384]{2,1,0:T(8,128)(2,1)}, u32[]{:S(2)}, u32[]{:S(2)}) async-start(bf16[8,128,384]{2,1,0:T(8,128)(2,1)} %bitcast.30), calls=%async_computation.3 | async-start | bytes 1572864 | tf_op jit(solution)/shard_map/all_to_all | solution.py:279
  148.0 2.6 %slice.50.query_ref = bf16[1024,640]{1,0:T(8,128)(2,1)} slice(bf16[1024,1024]{1,0:T(8,128)(2,1)} %bitcast.5), slice={[0:1024], [0:640]} | slice | bytes 2621440 | tf_op jit(solution)/shard_map/slice | solution.py:299
  151.7 43.1 %shard_map.56 = bf16[1024,640]{1,0:T(8,128)(2,1)} custom-call(s32[128,48]{1,0:T(8,128)S(1)} %copy-done.14, s32[128,8]{1,0:T(8,128)S(1)} %copy-done.15, bf16[1024,640]{1,0:T(8,128)(2,1)} %slice.50.query_ref, bf16[4096,128]{1,0:T(8,128)(2,1)} %constant_dynamic-update-slice_fusion.refs_0_, bf16[4096,128]{1,0:T(8,128)(2,1)S(1)} %collective-permute-done.8.refs_1_, ...), custom_call_target="tpu_custom_call" | custom-call | tf_op jit(solution)/shard_map/pallas_call | solution.py:163
  194.8 39.8 %all_to_all.21 = bf16[8,128,640]{2,1,0:T(8,128)(2,1)S(1)} all-to-all(bf16[8,128,640]{2,1,0:T(8,128)(2,1)} %bitcast.31), channel_id=1, replica_groups=mesh['z'=8,'x'=4,'core'=2,'rep'=4] {'z'}, dimensions={0} | all-to-all | bytes 2621440 | tf_op jit(solution)/shard_map/all_to_all | solution.py:279
  234.5 1.4 maximum_bitcast_fusion
  235.9 1.5 copy.16
  (95 shorter events, 24.4 us)
Async XLA Ops:
  27.9 6.4 %collective-permute-start = (bf16[1024,128]{1,0:T(8,128)(2,1)S(1)}, bf16[1024,128]{1,0:T(8,128)(2,1)S(1)}, u32[]{:S(2)}, u32[]{:S(2)}) collective-permute-start(bf16[1024,128]{1,0:T(8,128)(2,1)S(1)} %bitcast.36), channel_id=1, source_target_pairs={{0,8},{8,16},{16,24},{24,0},{1,9},{9,17},{17,25},{25,1},{2,10},{10... | collective-permute-start | bytes 786440 | tf_op jit(solution)/shard_map/ppermute | solution.py:182
  28.4 7.6 %collective-permute-start.1 = (bf16[1024,128]{1,0:T(8,128)(2,1)S(1)}, bf16[1024,128]{1,0:T(8,128)(2,1)S(1)}, u32[]{:S(2)}, u32[]{:S(2)}) collective-permute-start(bf16[1024,128]{1,0:T(8,128)(2,1)S(1)} %bitcast.37), channel_id=1, source_target_pairs={{0,24},{8,0},{16,8},{24,16},{1,25},{9,1},{17,9},{25,17},{2,26},{10... | collective-permute-start | bytes 786440 | tf_op jit(solution)/shard_map/ppermute | solution.py:182
  30.0 6.4 %collective-permute-start.2 = (bf16[1024,128]{1,0:T(8,128)(2,1)S(1)}, bf16[1024,128]{1,0:T(8,128)(2,1)S(1)}, u32[]{:S(2)}, u32[]{:S(2)}) collective-permute-start(bf16[1024,128]{1,0:T(8,128)(2,1)S(1)} %bitcast.33), channel_id=1, source_target_pairs={{0,1},{1,2},{2,3},{3,0},{4,5},{5,6},{6,7},{7,4},{8,9},{9,10},{10,1... | collective-permute-start | bytes 786440 | tf_op jit(solution)/shard_map/ppermute | solution.py:182
  30.2 7.6 %collective-permute-start.3 = (bf16[1024,128]{1,0:T(8,128)(2,1)S(1)}, bf16[1024,128]{1,0:T(8,128)(2,1)S(1)}, u32[]{:S(2)}, u32[]{:S(2)}) collective-permute-start(bf16[1024,128]{1,0:T(8,128)(2,1)S(1)} %bitcast.34), channel_id=1, source_target_pairs={{0,3},{1,0},{2,1},{3,2},{4,7},{5,4},{6,5},{7,6},{8,11},{9,8},{10,9... | collective-permute-start | bytes 786440 | tf_op jit(solution)/shard_map/ppermute | solution.py:182
  40.0 6.4 %collective-permute-start.4 = (bf16[512,128]{1,0:T(8,128)(2,1)S(1)}, bf16[512,128]{1,0:T(8,128)(2,1)S(1)}, u32[]{:S(2)}, u32[]{:S(2)}) collective-permute-start(bf16[512,128]{1,0:T(8,128)(2,1)S(1)} %slice.38), channel_id=1, source_target_pairs={{0,8},{8,16},{16,24},{24,0},{1,9},{9,17},{17,25},{25,1},{2,10},{10... | collective-permute-start | bytes 393224 | tf_op jit(solution)/shard_map/ppermute | solution.py:182
  41.7 6.2 %collective-permute-start.5 = (bf16[512,128]{1,0:T(8,128)(2,1)S(1)}, bf16[512,128]{1,0:T(8,128)(2,1)S(1)}, u32[]{:S(2)}, u32[]{:S(2)}) collective-permute-start(bf16[512,128]{1,0:T(8,128)(2,1)S(1)} %slice.39), channel_id=1, source_target_pairs={{0,24},{8,0},{16,8},{24,16},{1,25},{9,1},{17,9},{25,17},{2,26},{10... | collective-permute-start | bytes 393224 | tf_op jit(solution)/shard_map/ppermute | solution.py:182
  42.0 5.8 %collective-permute-start.6 = (bf16[512,128]{1,0:T(8,128)(2,1)S(1)}, bf16[512,128]{1,0:T(8,128)(2,1)S(1)}, u32[]{:S(2)}, u32[]{:S(2)}) collective-permute-start(bf16[512,128]{1,0:T(8,128)(2,1)S(1)} %slice.40), channel_id=1, source_target_pairs={{0,1},{1,2},{2,3},{3,0},{4,5},{5,6},{6,7},{7,4},{8,9},{9,10},{10,1... | collective-permute-start | bytes 393224 | tf_op jit(solution)/shard_map/ppermute | solution.py:182
  42.5 6.3 %collective-permute-start.7 = (bf16[512,128]{1,0:T(8,128)(2,1)S(1)}, bf16[512,128]{1,0:T(8,128)(2,1)S(1)}, u32[]{:S(2)}, u32[]{:S(2)}) collective-permute-start(bf16[512,128]{1,0:T(8,128)(2,1)S(1)} %slice.41), channel_id=1, source_target_pairs={{0,3},{1,0},{2,1},{3,2},{4,7},{5,4},{6,5},{7,6},{8,11},{9,8},{10,9... | collective-permute-start | bytes 393224 | tf_op jit(solution)/shard_map/ppermute | solution.py:182
  51.4 19.6 %collective-permute-start.8 = (bf16[4096,128]{1,0:T(8,128)(2,1)}, bf16[4096,128]{1,0:T(8,128)(2,1)S(1)}, u32[]{:S(2)}, u32[]{:S(2)}) collective-permute-start(bf16[4096,128]{1,0:T(8,128)(2,1)} %constant_dynamic-update-slice_fusion.refs_0_), channel_id=1, source_target_pairs={{0,1},{1,2},{2,3},{3,0},{4,5},{5,6},{6,7},{7,4},{8,9},{9,10},{10,1... | collective-permute-start | bytes 3145736 | tf_op jit(solution)/shard_map/ppermute | solution.py:182
  53.2 17.8 %copy-start.17 = (s32[64,24]{0,1:T(8,128)S(1)}, s32[64,24]{0,1:T(8,128)}, u32[]{:S(2)}) copy-start(s32[64,24]{0,1:T(8,128)} %param.8) | copy-start | bytes 18436
  53.2 18.5 %copy-start.18 = (s32[64,24]{0,1:T(8,128)S(1)}, s32[64,24]{0,1:T(8,128)}, u32[]{:S(2)}) copy-start(s32[64,24]{0,1:T(8,128)} %param.9) | copy-start | bytes 18436
  53.2 53.0 %all-to-all-start.1 = ((bf16[8,128,1024]{2,1,0:T(8,128)(2,1)}), bf16[8,128,1024]{2,1,0:T(8,128)(2,1)}, u32[]{:S(2)}, u32[]{:S(2)}) async-start(bf16[8,128,1024]{2,1,0:T(8,128)(2,1)} %bitcast.29), calls=%async_computation.1 | async-start | bytes 4194304 | tf_op jit(solution)/shard_map/all_to_all | solution.py:279
  57.7 20.7 %collective-permute-start.9 = (bf16[4096,128]{1,0:T(8,128)(2,1)}, bf16[4096,128]{1,0:T(8,128)(2,1)S(1)}, u32[]{:S(2)}, u32[]{:S(2)}) collective-permute-start(bf16[4096,128]{1,0:T(8,128)(2,1)} %constant_dynamic-update-slice_fusion.refs_0_), channel_id=1, source_target_pairs={{0,3},{1,0},{2,1},{3,2},{4,7},{5,4},{6,5},{7,6},{8,11},{9,8},{10,9... | collective-permute-start | bytes 3145736 | tf_op jit(solution)/shard_map/ppermute | solution.py:182
  59.5 19.6 %collective-permute-start.10 = (bf16[4096,128]{1,0:T(8,128)(2,1)}, bf16[4096,128]{1,0:T(8,128)(2,1)S(1)}, u32[]{:S(2)}, u32[]{:S(2)}) collective-permute-start(bf16[4096,128]{1,0:T(8,128)(2,1)} %constant_dynamic-update-slice_fusion.5.refs_10_), channel_id=1, source_target_pairs={{0,8},{8,16},{16,24},{24,0},{1,9},{9,17},{17,25},{25,1},{2,10},{10... | collective-permute-start | bytes 3145736 | tf_op jit(solution)/shard_map/ppermute | solution.py:182
  62.4 20.1 %collective-permute-start.11 = (bf16[4096,128]{1,0:T(8,128)(2,1)}, bf16[4096,128]{1,0:T(8,128)(2,1)}, u32[]{:S(2)}, u32[]{:S(2)}) collective-permute-start(bf16[4096,128]{1,0:T(8,128)(2,1)} %constant_dynamic-update-slice_fusion.5.refs_10_), channel_id=1, source_target_pairs={{0,24},{8,0},{16,8},{24,16},{1,25},{9,1},{17,9},{25,17},{2,26},{10... | collective-permute-start | bytes 3145736 | tf_op jit(solution)/shard_map/ppermute | solution.py:182
  62.4 20.1 %collective-permute-start.12 = (bf16[4096,128]{1,0:T(8,128)(2,1)}, bf16[4096,128]{1,0:T(8,128)(2,1)}, u32[]{:S(2)}, u32[]{:S(2)}) collective-permute-start(bf16[4096,128]{1,0:T(8,128)(2,1)} %constant_dynamic-update-slice_fusion.refs_0_), channel_id=1, source_target_pairs={{0,4},{4,0},{1,5},{5,1},{2,6},{6,2},{3,7},{7,3},{8,12},{12,8},{9,1... | collective-permute-start | bytes 3145736 | tf_op jit(solution)/shard_map/ppermute | solution.py:182
  71.0 11.5 %collective-permute-start.13 = (bf16[4096,128]{1,0:T(8,128)(2,1)}, bf16[4096,128]{1,0:T(8,128)(2,1)}, u32[]{:S(2)}, u32[]{:S(2)}) collective-permute-start(bf16[4096,128]{1,0:T(8,128)(2,1)} %constant_dynamic-update-slice_fusion.5.refs_10_), channel_id=1, source_target_pairs={{0,4},{4,0},{1,5},{5,1},{2,6},{6,2},{3,7},{7,3},{8,12},{12,8},{9,1... | collective-permute-start | bytes 3145736 | tf_op jit(solution)/shard_map/ppermute | solution.py:182
  82.5 9.5 %collective-permute-start.14 = (bf16[2048,128]{1,0:T(8,128)(2,1)S(1)}, bf16[2048,128]{1,0:T(8,128)(2,1)S(1)}, u32[]{:S(2)}, u32[]{:S(2)}) collective-permute-start(bf16[2048,128]{1,0:T(8,128)(2,1)S(1)} %slice.43), channel_id=1, source_target_pairs={{0,1},{1,2},{2,3},{3,0},{4,5},{5,6},{6,7},{7,4},{8,9},{9,10},{10,1... | collective-permute-start | bytes 1572872 | tf_op jit(solution)/shard_map/ppermute | solution.py:182
  84.5 17.9 %collective-permute-start.16 = (bf16[4096,128]{1,0:T(8,128)(2,1)S(1)}, bf16[4096,128]{1,0:T(8,128)(2,1)S(1)}, u32[]{:S(2)}, u32[]{:S(2)}) collective-permute-start(bf16[4096,128]{1,0:T(8,128)(2,1)S(1)} %collective-permute-done.8.refs_1_), channel_id=1, source_target_pairs={{0,4},{4,0},{1,5},{5,1},{2,6},{6,2},{3,7},{7,3},{8,12},{12,8},{9,1... | collective-permute-start | bytes 3145736 | tf_op jit(solution)/shard_map/ppermute | solution.py:182
  84.5 23.7 %copy-start.14 = (s32[128,48]{1,0:T(8,128)S(1)}, s32[128,48]{1,0:T(8,128)}, u32[]{:S(2)}) copy-start(s32[128,48]{1,0:T(8,128)} %get-tuple-element.48.idx_ref) | copy-start | bytes 73732
  84.5 23.7 %copy-start.15 = (s32[128,8]{1,0:T(8,128)S(1)}, s32[128,8]{1,0:T(8,128)}, u32[]{:S(2)}) copy-start(s32[128,8]{1,0:T(8,128)} %get-tuple-element.49.count_ref) | copy-start | bytes 12292
  84.5 15.7 %collective-permute-start.15 = (bf16[2048,128]{1,0:T(8,128)(2,1)S(1)}, bf16[2048,128]{1,0:T(8,128)(2,1)}, u32[]{:S(2)}, u32[]{:S(2)}) collective-permute-start(bf16[2048,128]{1,0:T(8,128)(2,1)S(1)} %slice.44), channel_id=1, source_target_pairs={{0,3},{1,0},{2,1},{3,2},{4,7},{5,4},{6,5},{7,6},{8,11},{9,8},{10,9... | collective-permute-start | bytes 1572872 | tf_op jit(solution)/shard_map/ppermute | solution.py:182
  84.8 15.5 %collective-permute-start.18 = (bf16[2048,128]{1,0:T(8,128)(2,1)S(1)}, bf16[2048,128]{1,0:T(8,128)(2,1)}, u32[]{:S(2)}, u32[]{:S(2)}) collective-permute-start(bf16[2048,128]{1,0:T(8,128)(2,1)S(1)} %slice.45), channel_id=1, source_target_pairs={{0,8},{8,16},{16,24},{24,0},{1,9},{9,17},{17,25},{25,1},{2,10},{10... | collective-permute-start | bytes 1572872 | tf_op jit(solution)/shard_map/ppermute | solution.py:182
  86.2 15.4 %collective-permute-start.19 = (bf16[2048,128]{1,0:T(8,128)(2,1)S(1)}, bf16[2048,128]{1,0:T(8,128)(2,1)}, u32[]{:S(2)}, u32[]{:S(2)}) collective-permute-start(bf16[2048,128]{1,0:T(8,128)(2,1)S(1)} %slice.46), channel_id=1, source_target_pairs={{0,24},{8,0},{16,8},{24,16},{1,25},{9,1},{17,9},{25,17},{2,26},{10... | collective-permute-start | bytes 1572872 | tf_op jit(solution)/shard_map/ppermute | solution.py:182
  92.0 11.9 %collective-permute-start.17 = (bf16[4096,128]{1,0:T(8,128)(2,1)S(1)}, bf16[4096,128]{1,0:T(8,128)(2,1)S(1)}, u32[]{:S(2)}, u32[]{:S(2)}) collective-permute-start(bf16[4096,128]{1,0:T(8,128)(2,1)S(1)} %collective-permute-done.9.refs_2_), channel_id=1, source_target_pairs={{0,4},{4,0},{1,5},{5,1},{2,6},{6,2},{3,7},{7,3},{8,12},{12,8},{9,1... | collective-permute-start | bytes 3145736 | tf_op jit(solution)/shard_map/ppermute | solution.py:182
  100.3 7.3 %collective-permute-start.22 = (bf16[4096,128]{1,0:T(8,128)(2,1)S(1)}, bf16[4096,128]{1,0:T(8,128)(2,1)}, u32[]{:S(2)}, u32[]{:S(2)}) collective-permute-start(bf16[4096,128]{1,0:T(8,128)(2,1)S(1)} %collective-permute-done.10.refs_11_), channel_id=1, source_target_pairs={{0,4},{4,0},{1,5},{5,1},{2,6},{6,2},{3,7},{7,3},{8,12},{12,8},{9,1... | collective-permute-start | bytes 3145736 | tf_op jit(solution)/shard_map/ppermute | solution.py:182
  100.3 7.3 %collective-permute-start.23 = (bf16[4096,128]{1,0:T(8,128)(2,1)}, bf16[4096,128]{1,0:T(8,128)(2,1)}, u32[]{:S(2)}, u32[]{:S(2)}) collective-permute-start(bf16[4096,128]{1,0:T(8,128)(2,1)} %collective-permute-done.11.refs_12_), channel_id=1, source_target_pairs={{0,4},{4,0},{1,5},{5,1},{2,6},{6,2},{3,7},{7,3},{8,12},{12,8},{9,1... | collective-permute-start | bytes 3145736 | tf_op jit(solution)/shard_map/ppermute | solution.py:182
  101.6 3.6 %collective-permute-start.20 = (bf16[2048,128]{1,0:T(8,128)(2,1)S(1)}, bf16[2048,128]{1,0:T(8,128)(2,1)S(1)}, u32[]{:S(2)}, u32[]{:S(2)}) collective-permute-start(bf16[2048,128]{1,0:T(8,128)(2,1)S(1)} %collective-permute-done.14.refs_3_), channel_id=1, source_target_pairs={{0,4},{4,0},{1,5},{5,1},{2,6},{6,2},{3,7},{7,3},{8,12},{12,8},{9,1... | collective-permute-start | bytes 1572872 | tf_op jit(solution)/shard_map/ppermute | solution.py:182
  103.4 4.1 %collective-permute-start.21 = (bf16[2048,128]{1,0:T(8,128)(2,1)}, bf16[2048,128]{1,0:T(8,128)(2,1)}, u32[]{:S(2)}, u32[]{:S(2)}) collective-permute-start(bf16[2048,128]{1,0:T(8,128)(2,1)} %collective-permute-done.15.refs_4_), channel_id=1, source_target_pairs={{0,4},{4,0},{1,5},{5,1},{2,6},{6,2},{3,7},{7,3},{8,12},{12,8},{9,1... | collective-permute-start | bytes 1572872 | tf_op jit(solution)/shard_map/ppermute | solution.py:182
  104.9 2.7 %collective-permute-start.24 = (bf16[2048,128]{1,0:T(8,128)(2,1)}, bf16[2048,128]{1,0:T(8,128)(2,1)}, u32[]{:S(2)}, u32[]{:S(2)}) collective-permute-start(bf16[2048,128]{1,0:T(8,128)(2,1)} %collective-permute-done.18.refs_13_), channel_id=1, source_target_pairs={{0,4},{4,0},{1,5},{5,1},{2,6},{6,2},{3,7},{7,3},{8,12},{12,8},{9,1... | collective-permute-start | bytes 1572872 | tf_op jit(solution)/shard_map/ppermute | solution.py:182
  106.0 2.3 collective-permute-start.25
  136.7 58.1 %all-to-all-start.3 = ((bf16[8,128,384]{2,1,0:T(8,128)(2,1)}), bf16[8,128,384]{2,1,0:T(8,128)(2,1)}, u32[]{:S(2)}, u32[]{:S(2)}) async-start(bf16[8,128,384]{2,1,0:T(8,128)(2,1)} %bitcast.30), calls=%async_computation.3 | async-start | bytes 1572864 | tf_op jit(solution)/shard_map/all_to_all | solution.py:279
  (15 other events, 32.3 us)
